TPU v7x, 768 devices: a whole 4x8x12 slice. The times are simulated.
768 devices in a mesh: energy: 24 (over y_lo, z), tile: 32 (over y_hi, x, core).
Axes of the slice: x: 4, y: 8 (y_hi: 4, y_lo: 2; y = y_hi * 2 + y_lo), z: 12, core: 2. Of those that a mesh axis runs over, the one named last changes fastest.
Arguments:
- g_less: bfloat16 [2, 768, 16384], P(None, 'energy', 'tile'), may hold values from -6 to 6
- g_great: bfloat16 [2, 768, 16384], P(None, 'energy', 'tile'), may hold values from -6 to 6
- coulomb: float32 [16384], P('tile'), may hold values from 0.3 to 3
- precond: bfloat16 [3, 16384, 512], P(None, 'tile'), may hold values from -0.25 to 0.25
Outputs:
- polar: float32 [768, 16384], P('energy', 'tile')
- screened: float32 [768, 16384], P('energy', 'tile')
All inputs are finite; a program needn't handle non-finite values.
Results may differ from a plain program's by a relative error of at most 0.008.
Values may be sent and summed in bfloat16 or wider, within the bound.
No kernel may reach another device: no remote copies, remote signals or barrier semaphores. Data moves between devices by JAX's collectives and lax.ppermute only.
A program may use at most 32 MiB of HBM per device.

v0:
```python
import math

import jax
import jax.numpy as jnp
from jax import lax
from jax.sharding import PartitionSpec as P

ITERS = 2


def padded_2(cells, sides, width):
    for axis, dim in sides:
        count = lax.axis_size(axis)
        ends = count - 1
        head = lax.slice_in_dim(cells, 0, width, axis=dim)
        tail = lax.slice_in_dim(cells, cells.shape[dim] - width, cells.shape[dim], axis=dim)
        cells = jnp.concatenate(
            [
                lax.ppermute(tail, axis, [(i, (i + 1) % count) for i in range(ends)]),
                cells,
                lax.ppermute(head, axis, [((i + 1) % count, i) for i in range(ends)]),
            ],
            axis=dim,
        )
    return cells


def per_device(g_less, g_great, coulomb, precond):
    e_dev = g_less.shape[1]
    order = g_less.shape[2]
    n_energy = lax.axis_size("energy")
    total = e_dev * n_energy
    first = lax.axis_index("energy") * e_dev
    empty = jnp.zeros((e_dev, order), jnp.float32)
    less_all, great_all = (
        lax.all_gather(g_less, "energy", axis=1, tiled=True),
        lax.all_gather(g_great, "energy", axis=1, tiled=True),
    )
    padded = jnp.concatenate([less_all, jnp.zeros_like(less_all)], axis=1)
    great_f = great_all.astype(jnp.float32)
    count = great_all.shape[1]

    def one_energy(shift, acc):
        offset = first + shift
        window = lax.dynamic_slice_in_dim(padded, offset, count, 1).astype(jnp.float32)
        value = jnp.sum(window[0] * great_f[0] - window[1] * great_f[1], axis=0)
        return acc.at[shift].add(value)

    summed = lax.fori_loop(0, e_dev, one_energy, empty)
    polar = summed * (0.25 / math.sqrt(total))
    bare = coulomb[None, :]
    screened = jnp.broadcast_to(bare, (e_dev, order))
    for step in range(ITERS):
        resid = bare - screened + bare * polar * screened
        resid_b = resid.astype(jnp.bfloat16)
        widened_rows = padded_2(resid_b, (("tile", 1),), order)
        before = widened_rows[:, :order]
        after = widened_rows[:, 2 * order :]
        product = jnp.dot(resid_b, precond[0], preferred_element_type=jnp.float32)
        product = product + jnp.dot(before, precond[1], preferred_element_type=jnp.float32)
        product = product + jnp.dot(after, precond[2], preferred_element_type=jnp.float32)
        corr = product.astype(jnp.bfloat16).astype(jnp.float32)
        screened = screened + 0.5 * resid + corr
    return (polar, screened)


def solution(mesh):
    placed = (
        P(None, "energy", "tile"),
        P(None, "energy", "tile"),
        P("tile"),
        P(None, "tile", None),
    )
    return jax.shard_map(
        per_device,
        mesh=mesh,
        in_specs=placed,
        out_specs=(P("energy", "tile"), P("energy", "tile")),
        check_vma=False,
    )
```

profile of v0, /device:TPU:23, one launch (start us, length us, event | category | flops | bytes accessed | tf_op | source)
XLA Modules:
  0.0 397.9 jit_solution(9583621644451910972)
XLA Ops:
  9.3 97.0 %all-gather.5.cloned.1.call-done = bf16[2,768,512]{2,1,0:T(8,128)(2,1)} async-done(((bf16[2,32,512]{2,1,0:T(8,128)(2,1)}), bf16[2,768,512]{2,1,0:T(8,128)(2,1)}) %all-gather.5.cloned.1.call-update) | async-done | bytes 1572880 | tf_op jit(solution)/shard_map/all_gather | solution.py:37
  108.3 100.7 %all-gather.3.cloned.1.call-done = bf16[2,768,512]{2,1,0:T(8,128)(2,1)} async-done(((bf16[2,32,512]{2,1,0:T(8,128)(2,1)}), bf16[2,768,512]{2,1,0:T(8,128)(2,1)}) %all-gather.3.cloned.1.call-update) | async-done | bytes 1572880 | tf_op jit(solution)/shard_map/all_gather | solution.py:36
  208.9 3.2 concatenate.11
  212.2 133.6 %while.14 = (s32[]{:T(128)}, f32[32,512]{1,0:T(8,128)S(1)}, s32[]{:T(128)}, bf16[2,1536,512]{2,1,0:T(8,128)(2,1)}, f32[2,768,512]{2,1,0:T(8,128)S(1)}, /*index=5...) while((s32[]{:T(128)}, f32[32,512]{1,0:T(8,128)S(1)}, s32[]{:T(128)}, ...), condition=%wide.region_3.0_spmd, body=%wide.region_0.0_spmd.sunk | while | flops 2359823 | bytes 11022521 | solution.py:49
  212.9 1.9 dynamic-slice_convert_fusion.2
  225.5 1.9 dynamic-slice_convert_fusion.2
  229.6 1.9 dynamic-slice_convert_fusion.2
  233.8 1.9 dynamic-slice_convert_fusion.2
  238.0 1.9 dynamic-slice_convert_fusion.2
  250.5 1.9 dynamic-slice_convert_fusion.2
  254.7 1.9 dynamic-slice_convert_fusion.2
  258.9 1.9 dynamic-slice_convert_fusion.2
  263.0 1.9 dynamic-slice_convert_fusion.2
  267.2 1.9 dynamic-slice_convert_fusion.2
  275.6 1.9 dynamic-slice_convert_fusion.2
  279.7 1.9 dynamic-slice_convert_fusion.2
  283.9 1.9 dynamic-slice_convert_fusion.2
  288.1 1.9 dynamic-slice_convert_fusion.2
  345.9 21.2 %collective-permute-start = (bf16[32,512]{1,0:T(8,128)(2,1)S(1)}, bf16[32,512]{1,0:T(8,128)(2,1)S(1)}, u32[]{:S(2)}, u32[]{:S(2)}) collective-permute-start(bf16[32,512]{1,0:T(8,128)(2,1)S(1)} %fusion.21), channel_id=1, source_target_pairs={{0,1},{1,2},{2,3},{3,4},{4,5},{5,6},{6,7},{7,8},{8,9},{9,10},{10,1... | collective-permute-start | bytes 98312 | tf_op jit(solution)/shard_map/ppermute | solution.py:19
  367.1 1.9 collective-permute-start.1
  371.5 5.1 %collective-permute-done.1 = bf16[32,512]{1,0:T(8,128)(2,1)S(1)} collective-permute-done((bf16[32,512]{1,0:T(8,128)(2,1)S(1)}, bf16[32,512]{1,0:T(8,128)(2,1)S(1)}, u32[]{:S(2)}, u32[]{:S(2)}) %collective-permute-start.1) | collective-permute-done | bytes 32800 | tf_op jit(solution)/shard_map/ppermute | solution.py:21
  377.8 2.8 collective-permute-start.2
  380.8 1.9 collective-permute-start.3
  382.9 7.3 %collective-permute-done.3 = bf16[32,512]{1,0:T(8,128)(2,1)S(1)} collective-permute-done((bf16[32,512]{1,0:T(8,128)(2,1)S(1)}, bf16[32,512]{1,0:T(8,128)(2,1)S(1)}, u32[]{:S(2)}, u32[]{:S(2)}) %collective-permute-start.3) | collective-permute-done | bytes 32800 | tf_op jit(solution)/shard_map/ppermute | solution.py:21
  (168 shorter events, 115.1 us)
Async XLA Ops:
  7.2 99.2 %all-gather.5.cloned.1.call-start = ((), (), s32[]{:S(2)}) async-start(), calls=%async_computation.1 | async-start | bytes 1638400 | tf_op jit(solution)/shard_map/all_gather | solution.py:37
  7.9 201.0 %all-gather.3.cloned.1.call-start = ((), (), s32[]{:S(2)}) async-start(), calls=%async_computation | async-start | bytes 1638400 | tf_op jit(solution)/shard_map/all_gather | solution.py:36
  108.2 103.9 %copy-start.2 = (s32[2]{0:T(128)S(1)}, s32[2]{0:T(128)}, u32[]{:S(2)}) copy-start(s32[2]{0:T(128)} %constant.81.clone.1) | copy-start | bytes 28
  212.2 133.6 %copy-start.1 = (f32[512]{0:T(512)S(1)}, f32[512]{0:T(512)}, u32[]{:S(2)}) copy-start(f32[512]{0:T(512)} %param.10) | copy-start | bytes 6148
  345.8 34.8 %copy-start = (bf16[3,512,512]{2,1,0:T(8,128)(2,1)S(1)}, bf16[3,512,512]{2,1,0:T(8,128)(2,1)}, u32[]{:S(2)}) copy-start(bf16[3,512,512]{2,1,0:T(8,128)(2,1)} %param.11) | copy-start | bytes 4718596
  345.9 24.4 %collective-permute-start = (bf16[32,512]{1,0:T(8,128)(2,1)S(1)}, bf16[32,512]{1,0:T(8,128)(2,1)S(1)}, u32[]{:S(2)}, u32[]{:S(2)}) collective-permute-start(bf16[32,512]{1,0:T(8,128)(2,1)S(1)} %fusion.21), channel_id=1, source_target_pairs={{0,1},{1,2},{2,3},{3,4},{4,5},{5,6},{6,7},{7,8},{8,9},{9,10},{10,1... | collective-permute-start | bytes 98312 | tf_op jit(solution)/shard_map/ppermute | solution.py:19
  367.1 9.5 %collective-permute-start.1 = (bf16[32,512]{1,0:T(8,128)(2,1)S(1)}, bf16[32,512]{1,0:T(8,128)(2,1)S(1)}, u32[]{:S(2)}, u32[]{:S(2)}) collective-permute-start(bf16[32,512]{1,0:T(8,128)(2,1)S(1)} %fusion.21), channel_id=1, source_target_pairs={{1,0},{2,1},{3,2},{4,3},{5,4},{6,5},{7,6},{8,7},{9,8},{10,9},{11,1... | collective-permute-start | bytes 98312 | tf_op jit(solution)/shard_map/ppermute | solution.py:21
  377.8 5.0 %collective-permute-start.2 = (bf16[32,512]{1,0:T(8,128)(2,1)S(1)}, bf16[32,512]{1,0:T(8,128)(2,1)S(1)}, u32[]{:S(2)}, u32[]{:S(2)}) collective-permute-start(bf16[32,512]{1,0:T(8,128)(2,1)S(1)} %get-tuple-element.133), channel_id=1, source_target_pairs={{0,1},{1,2},{2,3},{3,4},{4,5},{5,6},{6,7},{7,8},{8,9},{9,10},{10,1... | collective-permute-start | bytes 98312 | tf_op jit(solution)/shard_map/ppermute | solution.py:19
  380.8 9.5 %collective-permute-start.3 = (bf16[32,512]{1,0:T(8,128)(2,1)S(1)}, bf16[32,512]{1,0:T(8,128)(2,1)S(1)}, u32[]{:S(2)}, u32[]{:S(2)}) collective-permute-start(bf16[32,512]{1,0:T(8,128)(2,1)S(1)} %get-tuple-element.133), channel_id=1, source_target_pairs={{1,0},{2,1},{3,2},{4,3},{5,4},{6,5},{7,6},{8,7},{9,8},{10,9},{11,1... | collective-permute-start | bytes 98312 | tf_op jit(solution)/shard_map/ppermute | solution.py:21
Sparse Core Ops, SparseCore 0:
  10.4 95.9 all-gather.4
  108.8 100.0 all-gather.2
where the time goes:
time: 400 us; the launch traced here: 398 us
  waiting for transfers between devices  211 us (53%)
  other arithmetic  133 us (33%)
  starting transfers between devices  28 us (7%)
  between operations  14.2 us (4%)
  local copies, waits for them, and re-layouts  5.27 us (1%)
  matrix products  4.91 us (1%)
    all_gather x1, waiting for transfers between devices, per_device(): lax.all_gather(g_less, 'energy', axis=1, tiled=True)  101 us
    all_gather x1, waiting for transfers between devices, per_device(): lax.all_gather(g_great, 'energy', axis=1, tiled=True)  97 us
    convert_element_type x32, other arithmetic, one_energy(): lax.dynamic_slice_in_dim(padded, offset, count, 1).astype(jnp.float32)  59.8 us
    another operation x64, other arithmetic  44.1 us
    reduce_sum x32, other arithmetic, one_energy(): value = jnp.sum(window[0] * great_f[0] - window[1] * great_f[1], axis=0)  26.5 us
    ppermute x2, starting transfers between devices, padded_2(): lax.ppermute(tail, axis, [(i, (i + 1) % count) for i in range(ends)])  24 us
    ppermute x2, waiting for transfers between devices, padded_2(): lax.ppermute(head, axis, [((i + 1) % count, i) for i in range(ends)])  12.4 us
  transfers between devices with their start and end apart: 6, of which 4 were waited for; matrix products, arithmetic and copies ran while one was open for 1% of the time, Pallas kernels for 0%

commit v1 on v0

v1 whole, which is shorter than its diff:
```python
import math

import jax
import jax.numpy as jnp
import ml_dtypes
import numpy as np
from jax import lax
from jax.experimental import pallas as pl
from jax.experimental.pallas import tpu as pltpu
from jax.sharding import PartitionSpec as P

ITERS = 2
LANES = 128
VMEM_BYTES = 16 * 1024 * 1024
SLOT = 32


def dft_matrices(total):
    half = total // 2
    angle = 2.0 * np.pi / (2 * total)
    freq = np.arange(half)[:, None]
    rows = []
    for parity in (0, 1):
        at = 2 * np.arange(half)[None, :] + parity
        cos = np.cos(angle * ((freq * at) % (2 * total)))
        sin = np.sin(angle * ((freq * at) % (2 * total)))
        edge = (half * at[0]) % (2 * total)
        sin[0] = np.sin(angle * edge) if parity else np.cos(angle * edge)
        rows.append(np.concatenate([cos, sin], axis=0))
    return rows


def high_low(matrix):
    exact = matrix.astype(np.float32)
    high = exact.astype(ml_dtypes.bfloat16)
    low = (exact - high.astype(np.float32)).astype(ml_dtypes.bfloat16)
    return high, low


def pack_kernel(chunk, less_ref, great_ref, out_ref):
    e_dev, order = less_ref.shape[1], less_ref.shape[2]
    half = e_dev // 2
    row = lax.broadcasted_iota(jnp.int32, (4 * e_dev, 4 * e_dev), 0)
    col = lax.broadcasted_iota(jnp.int32, (4 * e_dev, 4 * e_dev), 1)
    inner = row % e_dev
    source = row - inner + jnp.where(inner < half, 2 * inner, 2 * (inner - half) + 1)
    select = jnp.where(col == source, 1.0, 0.0).astype(jnp.bfloat16)
    rows = jnp.concatenate([less_ref[0], less_ref[1], great_ref[0], great_ref[1]], axis=0)
    sorted_rows = jnp.dot(select, rows, preferred_element_type=jnp.float32)
    lane = lax.broadcasted_iota(jnp.int32, (e_dev, LANES), 1)
    for p in range(out_ref.shape[0]):
        low = chunk * p
        high = min(low + chunk, order) - 1
        first, last = low // LANES, high // LANES
        piece = None
        for q in range(4):
            shift = (SLOT * q - low) % LANES
            part = sorted_rows[e_dev * q : e_dev * (q + 1)]
            moved = pltpu.roll(part[:, LANES * first : LANES * (first + 1)], shift, 1)
            if last > first:
                after = pltpu.roll(part[:, LANES * last : LANES * (last + 1)], shift, 1)
                moved = jnp.where(lane >= SLOT * q + LANES * last - low, after, moved)
            piece = moved if q == 0 else jnp.where(lane >= SLOT * q, moved, piece)
        out_ref[p] = piece.astype(jnp.bfloat16)


def correlate_kernel(scale, data_ref, fwd_ref, back_ref, out_ref):
    blocks, e_dev, _ = data_ref.shape
    half = blocks * e_dev // 2
    spec = []
    for parity in (0, 1):
        rows = data_ref[:, parity * e_dev // 2 : (parity + 1) * e_dev // 2, :].reshape(half, LANES)
        full = jnp.dot(fwd_ref[2 * parity], rows, preferred_element_type=jnp.float32)
        full = full + jnp.dot(fwd_ref[2 * parity + 1], rows, preferred_element_type=jnp.float32)
        spec.append((full[:half], full[half:]))
    (ac_e, as_e), (ac_o, as_o) = spec
    bc_e, bs_e, bc_o, bs_o = (pltpu.roll(x, LANES // 2, 1) for x in (ac_e, as_e, ac_o, as_o))
    edge = lax.broadcasted_iota(jnp.int32, (half, LANES), 0) == 0
    cc = ac_e * bc_e + ac_o * bc_o
    ss = as_e * bs_e + as_o * bs_o
    even_c = jnp.where(edge, 0.5 * cc, cc + ss)
    even_s = jnp.where(edge, 0.5 * ss, as_e * bc_e + as_o * bc_o - ac_e * bs_e - ac_o * bs_o)
    cc = ac_e * bc_o + ac_o * bc_e
    odd_c = jnp.where(edge, 0.5 * cc, cc + as_e * bs_o + as_o * bs_e)
    odd_s = jnp.where(
        edge,
        0.5 * (as_o * bs_e - as_e * bs_o),
        as_e * bc_o + as_o * bc_e - ac_e * bs_o - ac_o * bs_e,
    )
    lane = lax.broadcasted_iota(jnp.int32, (blocks, 8, LANES), 2)
    result = None
    for parity, (c, s) in enumerate(((even_c, even_s), (odd_c, odd_s))):
        c = c - pltpu.roll(c, LANES - SLOT, 1)
        s = s - pltpu.roll(s, LANES - SLOT, 1)
        both = jnp.concatenate([c, s], axis=0).astype(jnp.bfloat16)
        lags = jnp.dot(back_ref[parity], both, preferred_element_type=jnp.float32) * scale
        lags = lags.reshape(blocks, 2, 8, LANES)
        for g in (0, 1):
            slot = 2 * parity + g
            part = lags[:, g]
            if slot == 0:
                result = part
            else:
                result = jnp.where(lane >= SLOT * slot, pltpu.roll(part, SLOT * slot, 2), result)
    out_ref[...] = result.astype(out_ref.dtype)


def store_in_order(sorted_rows, order_ref, out_ref):
    half = sorted_rows.shape[0] // 2
    for tile in range(order_ref.shape[0]):
        lanes = slice(LANES * tile, LANES * (tile + 1))
        order_ref[tile, pl.ds(0, half, stride=2), :] = sorted_rows[:half, lanes]
        order_ref[tile, pl.ds(1, half, stride=2), :] = sorted_rows[half:, lanes]
        out_ref[:, lanes] = order_ref[tile]


def unpack_kernel(chunk, data_ref, bare_ref, polar_ref, sorted_ref, resid_ref, order_ref):
    order = sorted_ref.shape[1]
    lane = lax.broadcasted_iota(jnp.int32, (8, LANES), 1)
    bare = bare_ref[...]
    for g in range(4):
        for tile in range(order // LANES):
            value = None
            p = (LANES * tile) // chunk
            while p < data_ref.shape[0] and chunk * p < LANES * (tile + 1):
                begin = chunk * p - LANES * tile
                moved = pltpu.roll(data_ref[p].astype(jnp.float32), (begin - SLOT * g) % LANES, 1)
                value = moved if value is None else jnp.where(lane >= begin, moved, value)
                p += 1
            lanes = slice(LANES * tile, LANES * (tile + 1))
            sorted_ref[8 * g : 8 * (g + 1), lanes] = value
    polar = sorted_ref[...]
    store_in_order(polar, order_ref, polar_ref)
    resid_ref[...] = (bare * polar * bare).astype(jnp.bfloat16)


def step_kernel(last, parity_ref, own_ref, chip_ref, far_ref, polar_ref, screened_ref, bare_ref, precond_ref, *out_refs):
    bare = bare_ref[...]
    polar = polar_ref[...]
    screened = screened_ref[...] if last else jnp.broadcast_to(bare, polar.shape)
    resid = bare - screened + bare * polar * screened
    even = parity_ref[0] == 0
    chip, far = chip_ref[...], far_ref[...]
    before = jnp.where(even, far, chip)
    after = jnp.where(even, chip, far)
    product = jnp.dot(own_ref[...], precond_ref[0], preferred_element_type=jnp.float32)
    product = product + jnp.dot(before, precond_ref[1], preferred_element_type=jnp.float32)
    product = product + jnp.dot(after, precond_ref[2], preferred_element_type=jnp.float32)
    corr = product.astype(jnp.bfloat16).astype(jnp.float32)
    screened = screened + 0.5 * resid + corr
    if last:
        store_in_order(screened, out_refs[1], out_refs[0])
    else:
        out_refs[0][...] = screened
        out_refs[1][...] = (bare - screened + bare * polar * screened).astype(jnp.bfloat16)


def per_device(g_less, g_great, coulomb, precond):
    e_dev, order = g_less.shape[1:]
    n_energy = lax.axis_size("energy")
    n_tile = lax.axis_size("tile")
    total = e_dev * n_energy
    chunk = -(-order // n_energy)
    vmem = pl.BlockSpec(memory_space=pltpu.VMEM)
    smem = pl.BlockSpec(memory_space=pltpu.SMEM)

    limit = pltpu.CompilerParams(vmem_limit_bytes=VMEM_BYTES)
    matrices = [high_low(m) for m in dft_matrices(total)]
    forward = jnp.asarray(np.stack([part for pair in matrices for part in pair]))
    backward = jnp.asarray(np.stack([np.ascontiguousarray(high.T) for high, _ in matrices]))

    pieces = pl.pallas_call(
        lambda *refs: pack_kernel(chunk, *refs),
        out_shape=jax.ShapeDtypeStruct((n_energy, e_dev, LANES), jnp.bfloat16),
        in_specs=[vmem, vmem],
        out_specs=vmem,
        compiler_params=limit,
    )(g_less, g_great)
    pieces = lax.all_to_all(pieces, "energy", 0, 0, tiled=True)
    scale = 0.25 / math.sqrt(total) * 4.0 / (2 * total)
    lags = pl.pallas_call(
        lambda *refs: correlate_kernel(scale, *refs),
        out_shape=jax.ShapeDtypeStruct((n_energy, 8, LANES), jnp.bfloat16),
        in_specs=[vmem] * 3,
        out_specs=vmem,
        compiler_params=limit,
    )(pieces, forward, backward)
    lags = lax.all_to_all(lags, "energy", 0, 0, tiled=True)
    bare = coulomb[None, :]
    plane = jax.ShapeDtypeStruct((e_dev, order), jnp.float32)
    plane_b = jax.ShapeDtypeStruct((e_dev, order), jnp.bfloat16)
    in_order = pltpu.VMEM((order // LANES, e_dev, LANES), jnp.float32)
    polar, polar_sorted, resid_b = pl.pallas_call(
        lambda *refs: unpack_kernel(chunk, *refs),
        out_shape=(plane, plane, plane_b),
        in_specs=[vmem] * 2,
        out_specs=(vmem,) * 3,
        scratch_shapes=[in_order],
        compiler_params=limit,
    )(lags, bare)
    parity = (lax.axis_index("tile") % 2).astype(jnp.int32).reshape(1)
    screened = polar_sorted
    chip_pairs = [(i, i ^ 1) for i in range(n_tile)]
    far_pairs = [(i, i + 1 if i % 2 else i - 1) for i in range(1, n_tile - 1)]
    for step in range(ITERS):
        last = step == ITERS - 1
        far = lax.ppermute(resid_b, "tile", far_pairs)
        chip = lax.ppermute(resid_b, "tile", chip_pairs)
        out = pl.pallas_call(
            lambda *refs, last=last: step_kernel(last, *refs),
            out_shape=(plane,) if last else (plane, plane_b),
            in_specs=[smem] + [vmem] * 7,
            out_specs=(vmem,) if last else (vmem, vmem),
            scratch_shapes=[in_order] if last else [],
            compiler_params=limit,
        )(parity, resid_b, chip, far, polar_sorted, screened, bare, precond)
        screened = out[0]
        resid_b = out[-1]
    return (polar, screened)


def solution(mesh):
    placed = (
        P(None, "energy", "tile"),
        P(None, "energy", "tile"),
        P("tile"),
        P(None, "tile", None),
    )
    return jax.shard_map(
        per_device,
        mesh=mesh,
        in_specs=placed,
        out_specs=(P("energy", "tile"), P("energy", "tile")),
        check_vma=False,
    )
```

time: 400 us -> 78.4 us (0.20)
  waiting for transfers between devices: 211 us -> 10.2 us
  other arithmetic: 133 us -> 0 us
  blocking collectives: 0 us -> 43.2 us
  between operations: 14.2 us -> 0.72 us
  starting transfers between devices: 28 us -> 15 us
  matrix products: 4.91 us -> 0 us
  Pallas kernels: 0 us -> 4.14 us
    all_gather x2 -> x0, waiting for transfers between devices: 198 us -> none  [the longest x1 101 us: per_device(): lax.all_gather(g_less, 'energy', axis=1, tiled=True)]
    convert_element_type x34 -> x0, other arithmetic: 61.6 us -> none  [the longest x32 59.8 us: one_energy(): lax.dynamic_slice_in_dim(padded, offset, count, 1).astype(jnp.float32)]
    another operation x64 -> x0, other arithmetic: 44.1 us -> none
    all_to_all x0 -> x2, blocking collectives: none -> 43.2 us  [the longest x1 27.9 us: per_device(): pieces = lax.all_to_all(pieces, 'energy', 0, 0, tiled=True)]
    reduce_sum x32 -> x0, other arithmetic: 26.5 us -> none  [one_energy(): value = jnp.sum(window[0] * great_f[0] - window[1] * great_f[1], axis=0)]
    ppermute x4, starting transfers between devices: 27.9 us -> 15 us  [the longest x2 8.68 us: per_device(): far = lax.ppermute(resid_b, 'tile', far_pairs)]
    dot_general x6 -> x0, matrix products: 4.91 us -> none  [the longest x2 2.08 us: per_device(): jnp.dot(after, precond[2], preferred_element_type=jnp.float32)]
    unnamed x6 -> x12, local copies, waits for them, and re-layouts: 0.02 us -> 4.61 us
  transfers between devices with their start and end apart: 6 -> 4, of which waited for: 4 -> 2; matrix products, arithmetic and copies ran while one was open for 1% -> 0% of each run, Pallas kernels for 0% -> 0%
where the time goes in v1:
time: 78.4 us; the launch traced here: 77.9 us
  blocking collectives  43.2 us (55%)
  starting transfers between devices  15 us (19%)
  waiting for transfers between devices  10.2 us (13%)
  local copies, waits for them, and re-layouts  4.61 us (6%)
  Pallas kernels  4.14 us (5%)
    all_to_all x1, blocking collectives, per_device(): pieces = lax.all_to_all(pieces, 'energy', 0, 0, tiled=True)  27.9 us
    all_to_all x1, blocking collectives, per_device(): lags = lax.all_to_all(lags, 'energy', 0, 0, tiled=True)  15.3 us
    ppermute x2, waiting for transfers between devices, per_device(): far = lax.ppermute(resid_b, 'tile', far_pairs)  10.2 us
    ppermute x2, starting transfers between devices, per_device(): far = lax.ppermute(resid_b, 'tile', far_pairs)  8.68 us
    ppermute x2, starting transfers between devices, per_device(): chip = lax.ppermute(resid_b, 'tile', chip_pairs)  6.37 us
    unnamed x12, local copies, waits for them, and re-layouts  4.61 us
  transfers between devices with their start and end apart: 4, of which 2 were waited for; matrix products, arithmetic and copies ran while one was open for 0% of the time, Pallas kernels for 0%

profile of v1, /device:TPU:23, one launch (start us, length us, event | category | flops | bytes accessed | tf_op | source)
XLA Modules:
  0.0 77.9 jit_solution(16384070683649892994)
XLA Ops:
  0.6 0.0 copy-start.3
  0.6 0.8 %copy-done.3 = bf16[2,32,512]{2,1,0:T(8,128)(2,1)S(1)} copy-done((bf16[2,32,512]{2,1,0:T(8,128)(2,1)S(1)}, bf16[2,32,512]{2,1,0:T(8,128)(2,1)}, u32[]{:S(2)}) %copy-start.3) | copy-done | bytes 65560
  1.5 0.0 copy-start.4
  1.5 0.8 %copy-done.4 = bf16[2,32,512]{2,1,0:T(8,128)(2,1)S(1)} copy-done((bf16[2,32,512]{2,1,0:T(8,128)(2,1)S(1)}, bf16[2,32,512]{2,1,0:T(8,128)(2,1)}, u32[]{:S(2)}) %copy-start.4) | copy-done | bytes 65560
  2.3 0.4 shard_map.77
  2.8 27.9 %all_to_all.10.refs_0_ = bf16[24,32,128]{2,1,0:T(8,128)(2,1)S(1)} all-to-all(bf16[24,32,128]{2,1,0:T(8,128)(2,1)S(1)} %shard_map.77), channel_id=1, replica_groups=mesh['energy'=24,'tile'=32] {'energy'}, dimensions={0} | all-to-all | bytes 393216 | tf_op jit(solution)/shard_map/all_to_all | solution.py:179
  30.7 0.0 copy-start.1
  30.7 1.7 %copy-done.1 = bf16[4,768,384]{2,1,0:T(8,128)(2,1)S(1)} copy-done((bf16[4,768,384]{2,1,0:T(8,128)(2,1)S(1)}, bf16[4,768,384]{2,1,0:T(8,128)(2,1)}, u32[]{:S(2)}) %copy-start.1) | copy-done | bytes 2359320
  32.3 1.3 %copy-done.2 = bf16[2,384,768]{2,1,0:T(8,128)(2,1)S(1)} copy-done((bf16[2,384,768]{2,1,0:T(8,128)(2,1)S(1)}, bf16[2,384,768]{2,1,0:T(8,128)(2,1)}, u32[]{:S(2)}) %copy-start.2) | copy-done | bytes 1179672
  33.6 1.5 %shard_map.78 = bf16[24,8,128]{2,1,0:T(8,128)(2,1)S(1)} custom-call(bf16[24,32,128]{2,1,0:T(8,128)(2,1)S(1)} %all_to_all.10.refs_0_, bf16[4,768,384]{2,1,0:T(8,128)(2,1)S(1)} %copy-done.1, bf16[2,384,768]{2,1,0:T(8,128)(2,1)S(1)} %copy-done.2), custom_call_target="tpu_custom_call" | custom-call | tf_op jit(solution)/shard_map/pallas_call | solution.py:181
  35.1 15.3 %all_to_all.11.refs_0_ = bf16[24,8,128]{2,1,0:T(8,128)(2,1)S(1)} all-to-all(bf16[24,8,128]{2,1,0:T(8,128)(2,1)S(1)} %shard_map.78), channel_id=1, replica_groups=mesh['energy'=24,'tile'=32] {'energy'}, dimensions={0} | all-to-all | bytes 98304 | tf_op jit(solution)/shard_map/all_to_all | solution.py:188
  50.5 0.0 copy-done.5
  50.5 0.8 %shard_map.79 = (f32[32,512]{1,0:T(8,128)}, f32[32,512]{1,0:T(8,128)S(1)}, bf16[32,512]{1,0:T(8,128)(2,1)S(1)}) custom-call(bf16[24,8,128]{2,1,0:T(8,128)(2,1)S(1)} %all_to_all.11.refs_0_, f32[1,512]{1,0:T(1,128)S(1)} %bitcast.2), custom_call_target="tpu_custom_call" | custom-call | tf_op jit(solution)/shard_map/pallas_call | solution.py:193
  51.2 4.4 %collective-permute-start = (bf16[32,512]{1,0:T(8,128)(2,1)S(1)}, bf16[32,512]{1,0:T(8,128)(2,1)S(1)}, u32[]{:S(2)}, u32[]{:S(2)}) collective-permute-start(bf16[32,512]{1,0:T(8,128)(2,1)S(1)} %get-tuple-element.8.refs_1_), channel_id=1, source_target_pairs={{0,1},{1,0},{2,3},{3,2},{4,5},{5,4},{6,7},{7,6},{8,9},{9,8},{10,11... | collective-permute-start | bytes 98312 | tf_op jit(solution)/shard_map/ppermute | solution.py:208
  55.7 4.3 %collective-permute-start.1 = (bf16[32,512]{1,0:T(8,128)(2,1)S(1)}, bf16[32,512]{1,0:T(8,128)(2,1)S(1)}, u32[]{:S(2)}, u32[]{:S(2)}) collective-permute-start(bf16[32,512]{1,0:T(8,128)(2,1)S(1)} %get-tuple-element.8.refs_1_), channel_id=1, source_target_pairs={{1,2},{2,1},{3,4},{4,3},{5,6},{6,5},{7,8},{8,7},{9,10},{10,9},{11,... | collective-permute-start | bytes 98312 | tf_op jit(solution)/shard_map/ppermute | solution.py:207
  60.1 0.0 collective-permute-done.refs_2_
  60.1 5.1 %collective-permute-done.1.refs_3_ = bf16[32,512]{1,0:T(8,128)(2,1)S(1)} collective-permute-done((bf16[32,512]{1,0:T(8,128)(2,1)S(1)}, bf16[32,512]{1,0:T(8,128)(2,1)S(1)}, u32[]{:S(2)}, u32[]{:S(2)}) %collective-permute-start.1) | collective-permute-done | bytes 32800 | tf_op jit(solution)/shard_map/ppermute | solution.py:207
  65.1 0.0 copy-done
  65.2 0.4 shard_map.80
  65.5 1.9 %collective-permute-start.2 = (bf16[32,512]{1,0:T(8,128)(2,1)S(1)}, bf16[32,512]{1,0:T(8,128)(2,1)S(1)}, u32[]{:S(2)}, u32[]{:S(2)}) collective-permute-start(bf16[32,512]{1,0:T(8,128)(2,1)S(1)} %get-tuple-element.10.refs_1_), channel_id=1, source_target_pairs={{0,1},{1,0},{2,3},{3,2},{4,5},{5,4},{6,7},{7,6},{8,9},{9,8},{10,11... | collective-permute-start | bytes 98312 | tf_op jit(solution)/shard_map/ppermute | solution.py:208
  67.5 4.3 %collective-permute-start.3 = (bf16[32,512]{1,0:T(8,128)(2,1)S(1)}, bf16[32,512]{1,0:T(8,128)(2,1)S(1)}, u32[]{:S(2)}, u32[]{:S(2)}) collective-permute-start(bf16[32,512]{1,0:T(8,128)(2,1)S(1)} %get-tuple-element.10.refs_1_), channel_id=1, source_target_pairs={{1,2},{2,1},{3,4},{4,3},{5,6},{6,5},{7,8},{8,7},{9,10},{10,9},{11,... | collective-permute-start | bytes 98312 | tf_op jit(solution)/shard_map/ppermute | solution.py:207
  71.8 0.0 collective-permute-done.2.refs_2_
  71.8 5.1 %collective-permute-done.3.refs_3_ = bf16[32,512]{1,0:T(8,128)(2,1)S(1)} collective-permute-done((bf16[32,512]{1,0:T(8,128)(2,1)S(1)}, bf16[32,512]{1,0:T(8,128)(2,1)S(1)}, u32[]{:S(2)}, u32[]{:S(2)}) %collective-permute-start.3) | collective-permute-done | bytes 32800 | tf_op jit(solution)/shard_map/ppermute | solution.py:207
  76.9 1.0 %shard_map.81 = f32[32,512]{1,0:T(8,128)} custom-call(s32[1]{0:T(128)} %bitcast.1.refs_0_, bf16[32,512]{1,0:T(8,128)(2,1)S(1)} %get-tuple-element.10.refs_1_, bf16[32,512]{1,0:T(8,128)(2,1)S(1)} %collective-permute-done.2.refs_2_, bf16[32,512]{1,0:T(8,128)(2,1)S(1)} %collective-permute-done.3.refs_3_, f32[32,512]{1,0:T(8,128)S(1)} %get-tuple-element.9.refs_4_.refs_5_, ...), custom_call_target="tpu_custom_call" | custom-call | tf_op jit(solution)/shard_map/pallas_call | solution.py:209
  (3 shorter events, 0.0 us)
Async XLA Ops:
  0.6 0.8 %copy-start.3 = (bf16[2,32,512]{2,1,0:T(8,128)(2,1)S(1)}, bf16[2,32,512]{2,1,0:T(8,128)(2,1)}, u32[]{:S(2)}) copy-start(bf16[2,32,512]{2,1,0:T(8,128)(2,1)} %refs_0_.1) | copy-start | bytes 196612
  1.5 0.8 %copy-start.4 = (bf16[2,32,512]{2,1,0:T(8,128)(2,1)S(1)}, bf16[2,32,512]{2,1,0:T(8,128)(2,1)}, u32[]{:S(2)}) copy-start(bf16[2,32,512]{2,1,0:T(8,128)(2,1)} %refs_1_.2) | copy-start | bytes 196612
  30.7 1.7 %copy-start.1 = (bf16[4,768,384]{2,1,0:T(8,128)(2,1)S(1)}, bf16[4,768,384]{2,1,0:T(8,128)(2,1)}, u32[]{:S(2)}) copy-start(bf16[4,768,384]{2,1,0:T(8,128)(2,1)} %constant.21.clone.refs_1_) | copy-start | bytes 7077892
  32.3 1.3 %copy-start.2 = (bf16[2,384,768]{2,1,0:T(8,128)(2,1)S(1)}, bf16[2,384,768]{2,1,0:T(8,128)(2,1)}, u32[]{:S(2)}) copy-start(bf16[2,384,768]{2,1,0:T(8,128)(2,1)} %constant.22.clone.refs_2_) | copy-start | bytes 3538948
  33.6 16.8 %copy-start.5 = (f32[512]{0:T(512)S(1)}, f32[512]{0:T(512)}, u32[]{:S(2)}) copy-start(f32[512]{0:T(512)} %param.8) | copy-start | bytes 6148
  33.6 31.5 %copy-start = (bf16[3,512,512]{2,1,0:T(8,128)(2,1)S(1)}, bf16[3,512,512]{2,1,0:T(8,128)(2,1)}, u32[]{:S(2)}) copy-start(bf16[3,512,512]{2,1,0:T(8,128)(2,1)} %refs_7_.3) | copy-start | bytes 4718596
  51.2 8.8 %collective-permute-start = (bf16[32,512]{1,0:T(8,128)(2,1)S(1)}, bf16[32,512]{1,0:T(8,128)(2,1)S(1)}, u32[]{:S(2)}, u32[]{:S(2)}) collective-permute-start(bf16[32,512]{1,0:T(8,128)(2,1)S(1)} %get-tuple-element.8.refs_1_), channel_id=1, source_target_pairs={{0,1},{1,0},{2,3},{3,2},{4,5},{5,4},{6,7},{7,6},{8,9},{9,8},{10,11... | collective-permute-start | bytes 98312 | tf_op jit(solution)/shard_map/ppermute | solution.py:208
  55.7 9.5 %collective-permute-start.1 = (bf16[32,512]{1,0:T(8,128)(2,1)S(1)}, bf16[32,512]{1,0:T(8,128)(2,1)S(1)}, u32[]{:S(2)}, u32[]{:S(2)}) collective-permute-start(bf16[32,512]{1,0:T(8,128)(2,1)S(1)} %get-tuple-element.8.refs_1_), channel_id=1, source_target_pairs={{1,2},{2,1},{3,4},{4,3},{5,6},{6,5},{7,8},{8,7},{9,10},{10,9},{11,... | collective-permute-start | bytes 98312 | tf_op jit(solution)/shard_map/ppermute | solution.py:207
  65.5 6.3 %collective-permute-start.2 = (bf16[32,512]{1,0:T(8,128)(2,1)S(1)}, bf16[32,512]{1,0:T(8,128)(2,1)S(1)}, u32[]{:S(2)}, u32[]{:S(2)}) collective-permute-start(bf16[32,512]{1,0:T(8,128)(2,1)S(1)} %get-tuple-element.10.refs_1_), channel_id=1, source_target_pairs={{0,1},{1,0},{2,3},{3,2},{4,5},{5,4},{6,7},{7,6},{8,9},{9,8},{10,11... | collective-permute-start | bytes 98312 | tf_op jit(solution)/shard_map/ppermute | solution.py:208
  67.5 9.5 %collective-permute-start.3 = (bf16[32,512]{1,0:T(8,128)(2,1)S(1)}, bf16[32,512]{1,0:T(8,128)(2,1)S(1)}, u32[]{:S(2)}, u32[]{:S(2)}) collective-permute-start(bf16[32,512]{1,0:T(8,128)(2,1)S(1)} %get-tuple-element.10.refs_1_), channel_id=1, source_target_pairs={{1,2},{2,1},{3,4},{4,3},{5,6},{6,5},{7,8},{8,7},{9,10},{10,9},{11,... | collective-permute-start | bytes 98312 | tf_op jit(solution)/shard_map/ppermute | solution.py:207

commit v2 on v1

--- a/solution.py
+++ b/solution.py
@@ -37,7 +37,15 @@
     return high, low
 
 
-def pack_kernel(chunk, less_ref, great_ref, out_ref):
+def pack_kernel(chunk, less_hbm, great_hbm, fwd_hbm, back_hbm, out_ref, fwd_ref, back_ref, less_ref, great_ref, sems):
+    copies = [
+        pltpu.make_async_copy(src, dst, sems.at[n])
+        for n, (src, dst) in enumerate(
+            ((less_hbm, less_ref), (great_hbm, great_ref), (fwd_hbm, fwd_ref), (back_hbm, back_ref))
+        )
+    ]
+    for copy in copies:
+        copy.start()
     e_dev, order = less_ref.shape[1], less_ref.shape[2]
     half = e_dev // 2
     row = lax.broadcasted_iota(jnp.int32, (4 * e_dev, 4 * e_dev), 0)
@@ -45,9 +53,13 @@
     inner = row % e_dev
     source = row - inner + jnp.where(inner < half, 2 * inner, 2 * (inner - half) + 1)
     select = jnp.where(col == source, 1.0, 0.0).astype(jnp.bfloat16)
+    lane = lax.broadcasted_iota(jnp.int32, (e_dev, LANES), 1)
+    in_slot = lax.broadcasted_iota(jnp.int32, (8, LANES), 1) % SLOT
+    spare = SLOT - chunk
+    copies[0].wait()
+    copies[1].wait()
     rows = jnp.concatenate([less_ref[0], less_ref[1], great_ref[0], great_ref[1]], axis=0)
     sorted_rows = jnp.dot(select, rows, preferred_element_type=jnp.float32)
-    lane = lax.broadcasted_iota(jnp.int32, (e_dev, LANES), 1)
     for p in range(out_ref.shape[0]):
         low = chunk * p
         high = min(low + chunk, order) - 1
@@ -61,15 +73,30 @@
                 after = pltpu.roll(part[:, LANES * last : LANES * (last + 1)], shift, 1)
                 moved = jnp.where(lane >= SLOT * q + LANES * last - low, after, moved)
             piece = moved if q == 0 else jnp.where(lane >= SLOT * q, moved, piece)
-        out_ref[p] = piece.astype(jnp.bfloat16)
-
-
-def correlate_kernel(scale, data_ref, fwd_ref, back_ref, out_ref):
-    blocks, e_dev, _ = data_ref.shape
-    half = blocks * e_dev // 2
+        rest = piece[24:]
+        full = [
+            jnp.where(in_slot < chunk, piece[8 * g : 8 * (g + 1)], pltpu.roll(rest, chunk - spare * g, 1))
+            for g in range(3)
+        ]
+        out_ref[p] = jnp.concatenate(full, axis=0).astype(jnp.bfloat16)
+    copies[2].wait()
+    copies[3].wait()
+
+
+def correlate_kernel(chunk, scale, data_ref, fwd_ref, back_ref, out_ref):
+    blocks = data_ref.shape[0]
+    half = fwd_ref.shape[2]
+    in_slot = lax.broadcasted_iota(jnp.int32, (blocks, 8, LANES), 2) % SLOT
+    spare = SLOT - chunk
+    packed = [data_ref[:, 8 * g : 8 * (g + 1), :].astype(jnp.float32) for g in range(3)]
+    rest = None
+    for g in range(3):
+        moved = pltpu.roll(packed[g], LANES - chunk + spare * g, 2)
+        rest = moved if g == 0 else jnp.where(in_slot >= spare * g, moved, rest)
     spec = []
     for parity in (0, 1):
-        rows = data_ref[:, parity * e_dev // 2 : (parity + 1) * e_dev // 2, :].reshape(half, LANES)
+        rows = packed[:2] if parity == 0 else [packed[2], rest]
+        rows = jnp.concatenate(rows, axis=1).reshape(half, LANES).astype(jnp.bfloat16)
         full = jnp.dot(fwd_ref[2 * parity], rows, preferred_element_type=jnp.float32)
         full = full + jnp.dot(fwd_ref[2 * parity + 1], rows, preferred_element_type=jnp.float32)
         spec.append((full[:half], full[half:]))
@@ -114,10 +141,9 @@
         out_ref[:, lanes] = order_ref[tile]
 
 
-def unpack_kernel(chunk, data_ref, bare_ref, polar_ref, sorted_ref, resid_ref, order_ref):
+def unpack_kernel(chunk, data_ref, bare_ref, sorted_ref, resid_ref):
     order = sorted_ref.shape[1]
     lane = lax.broadcasted_iota(jnp.int32, (8, LANES), 1)
-    bare = bare_ref[...]
     for g in range(4):
         for tile in range(order // LANES):
             value = None
@@ -127,11 +153,13 @@
                 moved = pltpu.roll(data_ref[p].astype(jnp.float32), (begin - SLOT * g) % LANES, 1)
                 value = moved if value is None else jnp.where(lane >= begin, moved, value)
                 p += 1
-            lanes = slice(LANES * tile, LANES * (tile + 1))
-            sorted_ref[8 * g : 8 * (g + 1), lanes] = value
-    polar = sorted_ref[...]
-    store_in_order(polar, order_ref, polar_ref)
-    resid_ref[...] = (bare * polar * bare).astype(jnp.bfloat16)
+            sorted_ref[8 * g : 8 * (g + 1), LANES * tile : LANES * (tile + 1)] = value
+    bare = bare_ref[...]
+    resid_ref[...] = (bare * sorted_ref[...] * bare).astype(jnp.bfloat16)
+
+
+def order_kernel(sorted_ref, out_ref, order_ref):
+    store_in_order(sorted_ref[...], order_ref, out_ref)
 
 
 def step_kernel(last, parity_ref, own_ref, chip_ref, far_ref, polar_ref, screened_ref, bare_ref, precond_ref, *out_refs):
@@ -169,17 +197,23 @@
     forward = jnp.asarray(np.stack([part for pair in matrices for part in pair]))
     backward = jnp.asarray(np.stack([np.ascontiguousarray(high.T) for high, _ in matrices]))
 
-    pieces = pl.pallas_call(
+    hbm = pl.BlockSpec(memory_space=pltpu.HBM)
+    pieces, forward, backward = pl.pallas_call(
         lambda *refs: pack_kernel(chunk, *refs),
-        out_shape=jax.ShapeDtypeStruct((n_energy, e_dev, LANES), jnp.bfloat16),
-        in_specs=[vmem, vmem],
-        out_specs=vmem,
-        compiler_params=limit,
-    )(g_less, g_great)
+        out_shape=(
+            jax.ShapeDtypeStruct((n_energy, 24, LANES), jnp.bfloat16),
+            jax.ShapeDtypeStruct(forward.shape, jnp.bfloat16),
+            jax.ShapeDtypeStruct(backward.shape, jnp.bfloat16),
+        ),
+        in_specs=[hbm] * 4,
+        out_specs=(vmem,) * 3,
+        scratch_shapes=[pltpu.VMEM(g_less.shape, jnp.bfloat16)] * 2 + [pltpu.SemaphoreType.DMA((4,))],
+        compiler_params=limit,
+    )(*(pltpu.with_memory_space_constraint(x, pltpu.HBM) for x in (g_less, g_great, forward, backward)))
     pieces = lax.all_to_all(pieces, "energy", 0, 0, tiled=True)
     scale = 0.25 / math.sqrt(total) * 4.0 / (2 * total)
     lags = pl.pallas_call(
-        lambda *refs: correlate_kernel(scale, *refs),
+        lambda *refs: correlate_kernel(chunk, scale, *refs),
         out_shape=jax.ShapeDtypeStruct((n_energy, 8, LANES), jnp.bfloat16),
         in_specs=[vmem] * 3,
         out_specs=vmem,
@@ -190,14 +224,22 @@
     plane = jax.ShapeDtypeStruct((e_dev, order), jnp.float32)
     plane_b = jax.ShapeDtypeStruct((e_dev, order), jnp.bfloat16)
     in_order = pltpu.VMEM((order // LANES, e_dev, LANES), jnp.float32)
-    polar, polar_sorted, resid_b = pl.pallas_call(
+    polar_sorted, resid_b = pl.pallas_call(
         lambda *refs: unpack_kernel(chunk, *refs),
-        out_shape=(plane, plane, plane_b),
+        out_shape=(plane, plane_b),
         in_specs=[vmem] * 2,
-        out_specs=(vmem,) * 3,
+        out_specs=(vmem,) * 2,
+        compiler_params=limit,
+    )(lags, bare)
+    polar = pl.pallas_call(
+        order_kernel,
+        out_shape=plane,
+        in_specs=[vmem],
+        out_specs=vmem,
         scratch_shapes=[in_order],
         compiler_params=limit,
-    )(lags, bare)
+        cost_estimate=pl.CostEstimate(flops=1000, bytes_accessed=1000, transcendentals=0),
+    )(polar_sorted)
     parity = (lax.axis_index("tile") % 2).astype(jnp.int32).reshape(1)
     screened = polar_sorted
     chip_pairs = [(i, i ^ 1) for i in range(n_tile)]

time: 78.4 us -> 73 us (0.931)
  local copies, waits for them, and re-layouts: 4.61 us -> 0.01 us
  blocking collectives: 43.2 us -> 41.4 us
  Pallas kernels: 4.14 us -> 5.8 us
    unnamed x12 -> x4, local copies, waits for them, and re-layouts: 4.61 us -> 0.01 us
    pallas_call x2 -> x3, Pallas kernels: 1.95 us -> 4.25 us  [the longest x1 2.1 us: per_device(): pl.pallas_call(lambda *refs: pack_kernel(chunk, *refs), out_shape=(jax.Sh...]
    all_to_all x1, blocking collectives: 27.9 us -> 26.5 us  [per_device(): pieces = lax.all_to_all(pieces, 'energy', 0, 0, tiled=True)]
  transfers between devices with their start and end apart: 4 -> 4, of which waited for: 2 -> 2; matrix products, arithmetic and copies ran while one was open for 0% -> 0% of each run, Pallas kernels for 0% -> 1%
where the time goes in v2:
time: 73 us; the launch traced here: 72.8 us
  blocking collectives  41.4 us (57%)
  starting transfers between devices  15.3 us (21%)
  waiting for transfers between devices  9.54 us (13%)
  Pallas kernels  5.8 us (8%)
    all_to_all x1, blocking collectives, per_device(): pieces = lax.all_to_all(pieces, 'energy', 0, 0, tiled=True)  26.5 us
    all_to_all x1, blocking collectives, per_device(): lags = lax.all_to_all(lags, 'energy', 0, 0, tiled=True)  14.9 us
    ppermute x2, waiting for transfers between devices, per_device(): far = lax.ppermute(resid_b, 'tile', far_pairs)  9.54 us
    ppermute x2, starting transfers between devices, per_device(): far = lax.ppermute(resid_b, 'tile', far_pairs)  8.68 us
    ppermute x2, starting transfers between devices, per_device(): chip = lax.ppermute(resid_b, 'tile', chip_pairs)  6.64 us
    pallas_call x1, Pallas kernels, per_device(): pl.pallas_call(lambda *refs: pack_kernel(chunk, *refs), out_shape=(jax.Sh...  2.1 us
    pallas_call x1, Pallas kernels, per_device(): pl.pallas_call(lambda *refs: correlate_kernel(chunk, scale, *refs), out_s...  1.51 us
  transfers between devices with their start and end apart: 4, of which 2 were waited for; matrix products, arithmetic and copies ran while one was open for 0% of the time, Pallas kernels for 1%

profile of v2, /device:TPU:23, one launch (start us, length us, event | category | flops | bytes accessed | tf_op | source)
XLA Modules:
  0.0 72.8 jit_solution(7265841370531702702)
XLA Ops:
  0.6 2.1 %shard_map.77 = (bf16[24,24,128]{2,1,0:T(8,128)(2,1)S(1)}, bf16[4,768,384]{2,1,0:T(8,128)(2,1)S(1)}, bf16[2,384,768]{2,1,0:T(8,128)(2,1)S(1)}) custom-call(bf16[2,32,512]{2,1,0:T(8,128)(2,1)} %refs_0_.1, bf16[2,32,512]{2,1,0:T(8,128)(2,1)} %refs_1_.1, bf16[4,768,384]{2,1,0:T(8,128)(2,1)} %constant.21.clone.refs_2_, bf16[2,384,768]{2,1,0:T(8,128)(2,1)} %constant.22.clone.refs_3_), custom_call_target="tpu_custom_call" | custom-call | tf_op jit(solution)/shard_map/pallas_call | solution.py:201
  2.7 26.5 %all_to_all.10.refs_0_ = bf16[24,24,128]{2,1,0:T(8,128)(2,1)S(1)} all-to-all(bf16[24,24,128]{2,1,0:T(8,128)(2,1)S(1)} %get-tuple-element.9), channel_id=1, replica_groups=mesh['energy'=24,'tile'=32] {'energy'}, dimensions={0} | all-to-all | bytes 294912 | tf_op jit(solution)/shard_map/all_to_all | solution.py:213
  29.2 0.0 copy-start.1
  29.2 0.0 copy-start
  29.2 1.5 %shard_map.78 = bf16[24,8,128]{2,1,0:T(8,128)(2,1)S(1)} custom-call(bf16[24,24,128]{2,1,0:T(8,128)(2,1)S(1)} %all_to_all.10.refs_0_, bf16[4,768,384]{2,1,0:T(8,128)(2,1)S(1)} %get-tuple-element.10.refs_1_, bf16[2,384,768]{2,1,0:T(8,128)(2,1)S(1)} %get-tuple-element.11.refs_2_), custom_call_target="tpu_custom_call" | custom-call | tf_op jit(solution)/shard_map/pallas_call | solution.py:215
  30.7 14.9 %all_to_all.11.refs_0_ = bf16[24,8,128]{2,1,0:T(8,128)(2,1)S(1)} all-to-all(bf16[24,8,128]{2,1,0:T(8,128)(2,1)S(1)} %shard_map.78), channel_id=1, replica_groups=mesh['energy'=24,'tile'=32] {'energy'}, dimensions={0} | all-to-all | bytes 98304 | tf_op jit(solution)/shard_map/all_to_all | solution.py:222
  45.6 0.0 copy-done.1
  45.7 0.1 shard_map.79
  45.8 4.7 %collective-permute-start = (bf16[32,512]{1,0:T(8,128)(2,1)S(1)}, bf16[32,512]{1,0:T(8,128)(2,1)S(1)}, u32[]{:S(2)}, u32[]{:S(2)}) collective-permute-start(bf16[32,512]{1,0:T(8,128)(2,1)S(1)} %get-tuple-element.13.refs_1_), channel_id=1, source_target_pairs={{0,1},{1,0},{2,3},{3,2},{4,5},{5,4},{6,7},{7,6},{8,9},{9,8},{10,11... | collective-permute-start | bytes 98312 | tf_op jit(solution)/shard_map/ppermute | solution.py:250
  50.5 4.3 %collective-permute-start.1 = (bf16[32,512]{1,0:T(8,128)(2,1)S(1)}, bf16[32,512]{1,0:T(8,128)(2,1)S(1)}, u32[]{:S(2)}, u32[]{:S(2)}) collective-permute-start(bf16[32,512]{1,0:T(8,128)(2,1)S(1)} %get-tuple-element.13.refs_1_), channel_id=1, source_target_pairs={{1,2},{2,1},{3,4},{4,3},{5,6},{6,5},{7,8},{8,7},{9,10},{10,9},{11,... | collective-permute-start | bytes 98312 | tf_op jit(solution)/shard_map/ppermute | solution.py:249
  54.9 0.0 collective-permute-done.refs_2_
  54.9 5.1 %collective-permute-done.1.refs_3_ = bf16[32,512]{1,0:T(8,128)(2,1)S(1)} collective-permute-done((bf16[32,512]{1,0:T(8,128)(2,1)S(1)}, bf16[32,512]{1,0:T(8,128)(2,1)S(1)}, u32[]{:S(2)}, u32[]{:S(2)}) %collective-permute-start.1) | collective-permute-done | bytes 32800 | tf_op jit(solution)/shard_map/ppermute | solution.py:249
  60.0 0.0 copy-done
  60.0 0.4 shard_map.81
  60.4 1.9 %collective-permute-start.2 = (bf16[32,512]{1,0:T(8,128)(2,1)S(1)}, bf16[32,512]{1,0:T(8,128)(2,1)S(1)}, u32[]{:S(2)}, u32[]{:S(2)}) collective-permute-start(bf16[32,512]{1,0:T(8,128)(2,1)S(1)} %get-tuple-element.14.refs_1_), channel_id=1, source_target_pairs={{0,1},{1,0},{2,3},{3,2},{4,5},{5,4},{6,7},{7,6},{8,9},{9,8},{10,11... | collective-permute-start | bytes 98312 | tf_op jit(solution)/shard_map/ppermute | solution.py:250
  62.3 4.3 %collective-permute-start.3 = (bf16[32,512]{1,0:T(8,128)(2,1)S(1)}, bf16[32,512]{1,0:T(8,128)(2,1)S(1)}, u32[]{:S(2)}, u32[]{:S(2)}) collective-permute-start(bf16[32,512]{1,0:T(8,128)(2,1)S(1)} %get-tuple-element.14.refs_1_), channel_id=1, source_target_pairs={{1,2},{2,1},{3,4},{4,3},{5,6},{6,5},{7,8},{8,7},{9,10},{10,9},{11,... | collective-permute-start | bytes 98312 | tf_op jit(solution)/shard_map/ppermute | solution.py:249
  66.7 0.6 shard_map.80
  67.3 0.0 collective-permute-done.2.refs_2_
  67.3 4.5 %collective-permute-done.3.refs_3_ = bf16[32,512]{1,0:T(8,128)(2,1)S(1)} collective-permute-done((bf16[32,512]{1,0:T(8,128)(2,1)S(1)}, bf16[32,512]{1,0:T(8,128)(2,1)S(1)}, u32[]{:S(2)}, u32[]{:S(2)}) %collective-permute-start.3) | collective-permute-done | bytes 32800 | tf_op jit(solution)/shard_map/ppermute | solution.py:249
  71.8 1.0 %shard_map.82 = f32[32,512]{1,0:T(8,128)} custom-call(s32[1]{0:T(128)} %bitcast.1.refs_0_, bf16[32,512]{1,0:T(8,128)(2,1)S(1)} %get-tuple-element.14.refs_1_, bf16[32,512]{1,0:T(8,128)(2,1)S(1)} %collective-permute-done.2.refs_2_, bf16[32,512]{1,0:T(8,128)(2,1)S(1)} %collective-permute-done.3.refs_3_, ...), custom_call_target="tpu_custom_call" | custom-call | tf_op jit(solution)/shard_map/pallas_call | solution.py:251
Async XLA Ops:
  29.2 16.5 %copy-start.1 = (f32[512]{0:T(512)S(1)}, f32[512]{0:T(512)}, u32[]{:S(2)}) copy-start(f32[512]{0:T(512)} %param.8) | copy-start | bytes 6148
  29.2 30.8 %copy-start = (bf16[3,512,512]{2,1,0:T(8,128)(2,1)S(1)}, bf16[3,512,512]{2,1,0:T(8,128)(2,1)}, u32[]{:S(2)}) copy-start(bf16[3,512,512]{2,1,0:T(8,128)(2,1)} %refs_7_.3) | copy-start | bytes 4718596
  45.8 9.1 %collective-permute-start = (bf16[32,512]{1,0:T(8,128)(2,1)S(1)}, bf16[32,512]{1,0:T(8,128)(2,1)S(1)}, u32[]{:S(2)}, u32[]{:S(2)}) collective-permute-start(bf16[32,512]{1,0:T(8,128)(2,1)S(1)} %get-tuple-element.13.refs_1_), channel_id=1, source_target_pairs={{0,1},{1,0},{2,3},{3,2},{4,5},{5,4},{6,7},{7,6},{8,9},{9,8},{10,11... | collective-permute-start | bytes 98312 | tf_op jit(solution)/shard_map/ppermute | solution.py:250
  50.5 9.5 %collective-permute-start.1 = (bf16[32,512]{1,0:T(8,128)(2,1)S(1)}, bf16[32,512]{1,0:T(8,128)(2,1)S(1)}, u32[]{:S(2)}, u32[]{:S(2)}) collective-permute-start(bf16[32,512]{1,0:T(8,128)(2,1)S(1)} %get-tuple-element.13.refs_1_), channel_id=1, source_target_pairs={{1,2},{2,1},{3,4},{4,3},{5,6},{6,5},{7,8},{8,7},{9,10},{10,9},{11,... | collective-permute-start | bytes 98312 | tf_op jit(solution)/shard_map/ppermute | solution.py:249
  60.4 6.9 %collective-permute-start.2 = (bf16[32,512]{1,0:T(8,128)(2,1)S(1)}, bf16[32,512]{1,0:T(8,128)(2,1)S(1)}, u32[]{:S(2)}, u32[]{:S(2)}) collective-permute-start(bf16[32,512]{1,0:T(8,128)(2,1)S(1)} %get-tuple-element.14.refs_1_), channel_id=1, source_target_pairs={{0,1},{1,0},{2,3},{3,2},{4,5},{5,4},{6,7},{7,6},{8,9},{9,8},{10,11... | collective-permute-start | bytes 98312 | tf_op jit(solution)/shard_map/ppermute | solution.py:250
  62.3 9.5 %collective-permute-start.3 = (bf16[32,512]{1,0:T(8,128)(2,1)S(1)}, bf16[32,512]{1,0:T(8,128)(2,1)S(1)}, u32[]{:S(2)}, u32[]{:S(2)}) collective-permute-start(bf16[32,512]{1,0:T(8,128)(2,1)S(1)} %get-tuple-element.14.refs_1_), channel_id=1, source_target_pairs={{1,2},{2,1},{3,4},{4,3},{5,6},{6,5},{7,8},{8,7},{9,10},{10,9},{11,... | collective-permute-start | bytes 98312 | tf_op jit(solution)/shard_map/ppermute | solution.py:249

commit v3 on v2

--- a/solution.py
+++ b/solution.py
@@ -37,11 +37,11 @@
     return high, low
 
 
-def pack_kernel(chunk, less_hbm, great_hbm, fwd_hbm, back_hbm, out_ref, fwd_ref, back_ref, less_ref, great_ref, sems):
+def pack_kernel(chunk, less_hbm, great_hbm, fwd_hbm, out_ref, fwd_ref, less_ref, great_ref, sems):
     copies = [
         pltpu.make_async_copy(src, dst, sems.at[n])
         for n, (src, dst) in enumerate(
-            ((less_hbm, less_ref), (great_hbm, great_ref), (fwd_hbm, fwd_ref), (back_hbm, back_ref))
+            ((less_hbm, less_ref), (great_hbm, great_ref), (fwd_hbm, fwd_ref))
         )
     ]
     for copy in copies:
@@ -80,12 +80,13 @@
         ]
         out_ref[p] = jnp.concatenate(full, axis=0).astype(jnp.bfloat16)
     copies[2].wait()
-    copies[3].wait()
-
-
-def correlate_kernel(chunk, scale, data_ref, fwd_ref, back_ref, out_ref):
+
+
+def correlate_kernel(chunk, scale, data_ref, fwd_ref, back_hbm, out_ref, back_ref, sem):
+    copy = pltpu.make_async_copy(back_hbm, back_ref, sem)
+    copy.start()
     blocks = data_ref.shape[0]
-    half = fwd_ref.shape[2]
+    half = fwd_ref.shape[2] // 2
     in_slot = lax.broadcasted_iota(jnp.int32, (blocks, 8, LANES), 2) % SLOT
     spare = SLOT - chunk
     packed = [data_ref[:, 8 * g : 8 * (g + 1), :].astype(jnp.float32) for g in range(3)]
@@ -97,8 +98,8 @@
     for parity in (0, 1):
         rows = packed[:2] if parity == 0 else [packed[2], rest]
         rows = jnp.concatenate(rows, axis=1).reshape(half, LANES).astype(jnp.bfloat16)
-        full = jnp.dot(fwd_ref[2 * parity], rows, preferred_element_type=jnp.float32)
-        full = full + jnp.dot(fwd_ref[2 * parity + 1], rows, preferred_element_type=jnp.float32)
+        rows = jnp.concatenate([rows, rows], axis=0)
+        full = jnp.dot(fwd_ref[parity], rows, preferred_element_type=jnp.float32)
         spec.append((full[:half], full[half:]))
     (ac_e, as_e), (ac_o, as_o) = spec
     bc_e, bs_e, bc_o, bs_o = (pltpu.roll(x, LANES // 2, 1) for x in (ac_e, as_e, ac_o, as_o))
@@ -116,6 +117,7 @@
     )
     lane = lax.broadcasted_iota(jnp.int32, (blocks, 8, LANES), 2)
     result = None
+    copy.wait()
     for parity, (c, s) in enumerate(((even_c, even_s), (odd_c, odd_s))):
         c = c - pltpu.roll(c, LANES - SLOT, 1)
         s = s - pltpu.roll(s, LANES - SLOT, 1)
@@ -132,13 +134,26 @@
     out_ref[...] = result.astype(out_ref.dtype)
 
 
-def store_in_order(sorted_rows, order_ref, out_ref):
+def tile_copy(refs, tile):
+    out_hbm, order_ref, sems = refs
+    return pltpu.make_async_copy(
+        order_ref.at[tile], out_hbm.at[:, LANES * tile : LANES * (tile + 1)], sems.at[tile]
+    )
+
+
+def store_in_order(sorted_rows, refs, at):
     half = sorted_rows.shape[0] // 2
-    for tile in range(order_ref.shape[0]):
-        lanes = slice(LANES * tile, LANES * (tile + 1))
-        order_ref[tile, pl.ds(0, half, stride=2), :] = sorted_rows[:half, lanes]
-        order_ref[tile, pl.ds(1, half, stride=2), :] = sorted_rows[half:, lanes]
-        out_ref[:, lanes] = order_ref[tile]
+    for n in range(sorted_rows.shape[1] // LANES):
+        lanes = slice(LANES * n, LANES * (n + 1))
+        tile = at // LANES + n
+        refs[1][tile, pl.ds(0, half, stride=2), :] = sorted_rows[:half, lanes]
+        refs[1][tile, pl.ds(1, half, stride=2), :] = sorted_rows[half:, lanes]
+        tile_copy(refs, tile).start()
+
+
+def wait_in_order(refs):
+    for tile in range(refs[1].shape[0]):
+        tile_copy(refs, tile).wait()
 
 
 def unpack_kernel(chunk, data_ref, bare_ref, sorted_ref, resid_ref):
@@ -158,29 +173,37 @@
     resid_ref[...] = (bare * sorted_ref[...] * bare).astype(jnp.bfloat16)
 
 
-def order_kernel(sorted_ref, out_ref, order_ref):
-    store_in_order(sorted_ref[...], order_ref, out_ref)
-
-
-def step_kernel(last, parity_ref, own_ref, chip_ref, far_ref, polar_ref, screened_ref, bare_ref, precond_ref, *out_refs):
-    bare = bare_ref[...]
-    polar = polar_ref[...]
-    screened = screened_ref[...] if last else jnp.broadcast_to(bare, polar.shape)
-    resid = bare - screened + bare * polar * screened
-    even = parity_ref[0] == 0
-    chip, far = chip_ref[...], far_ref[...]
-    before = jnp.where(even, far, chip)
-    after = jnp.where(even, chip, far)
-    product = jnp.dot(own_ref[...], precond_ref[0], preferred_element_type=jnp.float32)
-    product = product + jnp.dot(before, precond_ref[1], preferred_element_type=jnp.float32)
-    product = product + jnp.dot(after, precond_ref[2], preferred_element_type=jnp.float32)
-    corr = product.astype(jnp.bfloat16).astype(jnp.float32)
-    screened = screened + 0.5 * resid + corr
+def order_kernel(sorted_ref, *refs):
+    store_in_order(sorted_ref[...], refs, 0)
+    wait_in_order(refs)
+
+
+def near_kernel(parity_ref, own_ref, chip_ref, precond_ref, out_ref):
+    which = 2 - parity_ref[0]
+    out_ref[...] = jnp.dot(own_ref[...], precond_ref[0], preferred_element_type=jnp.float32) + jnp.dot(
+        chip_ref[...], precond_ref[which], preferred_element_type=jnp.float32
+    )
+
+
+def step_kernel(last, parity_ref, near_ref, far_ref, polar_ref, screened_ref, bare_ref, precond_ref, *refs):
+    which = 1 + parity_ref[0]
+    far = far_ref[...]
+    width = 256 if last else far.shape[1]
+    for at in range(0, far.shape[1], width):
+        lanes = slice(at, at + width)
+        bare, polar = bare_ref[:, lanes], polar_ref[:, lanes]
+        screened = screened_ref[:, lanes] if last else jnp.broadcast_to(bare, polar.shape)
+        resid = bare - screened + bare * polar * screened
+        product = near_ref[:, lanes] + jnp.dot(far, precond_ref[which, :, lanes], preferred_element_type=jnp.float32)
+        corr = product.astype(jnp.bfloat16).astype(jnp.float32)
+        screened = screened + 0.5 * resid + corr
+        if last:
+            store_in_order(screened, refs, at)
+        else:
+            refs[0][:, lanes] = screened
+            refs[1][:, lanes] = (bare - screened + bare * polar * screened).astype(jnp.bfloat16)
     if last:
-        store_in_order(screened, out_refs[1], out_refs[0])
-    else:
-        out_refs[0][...] = screened
-        out_refs[1][...] = (bare - screened + bare * polar * screened).astype(jnp.bfloat16)
+        wait_in_order(refs)
 
 
 def per_device(g_less, g_great, coulomb, precond):
@@ -194,36 +217,42 @@
 
     limit = pltpu.CompilerParams(vmem_limit_bytes=VMEM_BYTES)
     matrices = [high_low(m) for m in dft_matrices(total)]
-    forward = jnp.asarray(np.stack([part for pair in matrices for part in pair]))
+    forward = jnp.asarray(np.stack([np.concatenate(pair, axis=1) for pair in matrices]))
     backward = jnp.asarray(np.stack([np.ascontiguousarray(high.T) for high, _ in matrices]))
 
     hbm = pl.BlockSpec(memory_space=pltpu.HBM)
-    pieces, forward, backward = pl.pallas_call(
+    g_less, g_great, forward, backward = (
+        pltpu.with_memory_space_constraint(x, pltpu.HBM) for x in (g_less, g_great, forward, backward)
+    )
+    pieces, forward = pl.pallas_call(
         lambda *refs: pack_kernel(chunk, *refs),
         out_shape=(
             jax.ShapeDtypeStruct((n_energy, 24, LANES), jnp.bfloat16),
             jax.ShapeDtypeStruct(forward.shape, jnp.bfloat16),
-            jax.ShapeDtypeStruct(backward.shape, jnp.bfloat16),
         ),
-        in_specs=[hbm] * 4,
-        out_specs=(vmem,) * 3,
-        scratch_shapes=[pltpu.VMEM(g_less.shape, jnp.bfloat16)] * 2 + [pltpu.SemaphoreType.DMA((4,))],
+        in_specs=[hbm] * 3,
+        out_specs=(vmem,) * 2,
+        scratch_shapes=[pltpu.VMEM(g_less.shape, jnp.bfloat16)] * 2 + [pltpu.SemaphoreType.DMA((3,))],
         compiler_params=limit,
-    )(*(pltpu.with_memory_space_constraint(x, pltpu.HBM) for x in (g_less, g_great, forward, backward)))
+    )(g_less, g_great, forward)
     pieces = lax.all_to_all(pieces, "energy", 0, 0, tiled=True)
     scale = 0.25 / math.sqrt(total) * 4.0 / (2 * total)
     lags = pl.pallas_call(
         lambda *refs: correlate_kernel(chunk, scale, *refs),
         out_shape=jax.ShapeDtypeStruct((n_energy, 8, LANES), jnp.bfloat16),
-        in_specs=[vmem] * 3,
+        in_specs=[vmem, vmem, hbm],
         out_specs=vmem,
+        scratch_shapes=[pltpu.VMEM(backward.shape, jnp.bfloat16), pltpu.SemaphoreType.DMA(())],
         compiler_params=limit,
     )(pieces, forward, backward)
     lags = lax.all_to_all(lags, "energy", 0, 0, tiled=True)
     bare = coulomb[None, :]
     plane = jax.ShapeDtypeStruct((e_dev, order), jnp.float32)
     plane_b = jax.ShapeDtypeStruct((e_dev, order), jnp.bfloat16)
-    in_order = pltpu.VMEM((order // LANES, e_dev, LANES), jnp.float32)
+    in_order = [
+        pltpu.VMEM((order // LANES, e_dev, LANES), jnp.float32),
+        pltpu.SemaphoreType.DMA((order // LANES,)),
+    ]
     polar_sorted, resid_b = pl.pallas_call(
         lambda *refs: unpack_kernel(chunk, *refs),
         out_shape=(plane, plane_b),
@@ -235,8 +264,8 @@
         order_kernel,
         out_shape=plane,
         in_specs=[vmem],
-        out_specs=vmem,
-        scratch_shapes=[in_order],
+        out_specs=hbm,
+        scratch_shapes=in_order,
         compiler_params=limit,
         cost_estimate=pl.CostEstimate(flops=1000, bytes_accessed=1000, transcendentals=0),
     )(polar_sorted)
@@ -248,14 +277,21 @@
         last = step == ITERS - 1
         far = lax.ppermute(resid_b, "tile", far_pairs)
         chip = lax.ppermute(resid_b, "tile", chip_pairs)
+        near = pl.pallas_call(
+            near_kernel,
+            out_shape=plane,
+            in_specs=[smem] + [vmem] * 3,
+            out_specs=vmem,
+            compiler_params=limit,
+        )(parity, resid_b, chip, precond)
         out = pl.pallas_call(
             lambda *refs, last=last: step_kernel(last, *refs),
             out_shape=(plane,) if last else (plane, plane_b),
-            in_specs=[smem] + [vmem] * 7,
-            out_specs=(vmem,) if last else (vmem, vmem),
-            scratch_shapes=[in_order] if last else [],
+            in_specs=[smem] + [vmem] * 6,
+            out_specs=(hbm,) if last else (vmem, vmem),
+            scratch_shapes=in_order if last else [],
             compiler_params=limit,
-        )(parity, resid_b, chip, far, polar_sorted, screened, bare, precond)
+        )(parity, near, far, polar_sorted, screened, bare, precond)
         screened = out[0]
         resid_b = out[-1]
     return (polar, screened)

time: 73 us -> 73.8 us (1.011)
  Pallas kernels: 5.8 us -> 6.86 us
    pallas_call x1, Pallas kernels: 1.51 us -> 2.66 us  [per_device(): pl.pallas_call(lambda *refs: correlate_kernel(chunk, scale, *refs), out_s...]
  transfers between devices with their start and end apart: 4 -> 4, of which waited for: 2 -> 2; matrix products, arithmetic and copies ran while one was open for 0% -> 0% of each run, Pallas kernels for 1% -> 2%
where the time goes in v3:
time: 73.8 us; the launch traced here: 73.4 us
  blocking collectives  41.5 us (56%)
  starting transfers between devices  15.3 us (21%)
  waiting for transfers between devices  8.95 us (12%)
  Pallas kernels  6.86 us (9%)
  between operations  0.75 us (1%)
    all_to_all x1, blocking collectives, per_device(): pieces = lax.all_to_all(pieces, 'energy', 0, 0, tiled=True)  26.6 us
    all_to_all x1, blocking collectives, per_device(): lags = lax.all_to_all(lags, 'energy', 0, 0, tiled=True)  14.9 us
    ppermute x2, waiting for transfers between devices, per_device(): far = lax.ppermute(resid_b, 'tile', far_pairs)  8.94 us
    ppermute x2, starting transfers between devices, per_device(): far = lax.ppermute(resid_b, 'tile', far_pairs)  8.68 us
    ppermute x2, starting transfers between devices, per_device(): chip = lax.ppermute(resid_b, 'tile', chip_pairs)  6.64 us
    pallas_call x1, Pallas kernels, per_device(): pl.pallas_call(lambda *refs: correlate_kernel(chunk, scale, *refs), out_s...  2.66 us
    pallas_call x1, Pallas kernels, per_device(): pl.pallas_call(lambda *refs: pack_kernel(chunk, *refs), out_shape=(jax.Sh...  1.77 us
  transfers between devices with their start and end apart: 4, of which 2 were waited for; matrix products, arithmetic and copies ran while one was open for 0% of the time, Pallas kernels for 2%

profile of v3, /device:TPU:23, one launch (start us, length us, event | category | flops | bytes accessed | tf_op | source)
XLA Modules:
  0.0 73.4 jit_solution(13035626078556341054)
XLA Ops:
  0.6 1.8 %shard_map.77 = (bf16[24,24,128]{2,1,0:T(8,128)(2,1)S(1)}, bf16[2,768,768]{2,1,0:T(8,128)(2,1)S(1)}) custom-call(bf16[2,32,512]{2,1,0:T(8,128)(2,1)} %refs_0_.1, bf16[2,32,512]{2,1,0:T(8,128)(2,1)} %refs_1_.1, bf16[2,768,768]{2,1,0:T(8,128)(2,1)} %constant.21.clone.refs_2_), custom_call_target="tpu_custom_call" | custom-call | tf_op jit(solution)/shard_map/pallas_call | solution.py:227
  2.4 0.0 copy-start.1
  2.4 0.0 copy-start
  2.4 26.6 %all_to_all.10.refs_0_ = bf16[24,24,128]{2,1,0:T(8,128)(2,1)S(1)} all-to-all(bf16[24,24,128]{2,1,0:T(8,128)(2,1)S(1)} %get-tuple-element.8), channel_id=1, replica_groups=mesh['energy'=24,'tile'=32] {'energy'}, dimensions={0} | all-to-all | bytes 294912 | tf_op jit(solution)/shard_map/all_to_all | solution.py:238
  29.0 2.7 %shard_map.78 = bf16[24,8,128]{2,1,0:T(8,128)(2,1)S(1)} custom-call(bf16[24,24,128]{2,1,0:T(8,128)(2,1)S(1)} %all_to_all.10.refs_0_, bf16[2,768,768]{2,1,0:T(8,128)(2,1)S(1)} %get-tuple-element.9.refs_1_, bf16[2,384,768]{2,1,0:T(8,128)(2,1)} %constant.22.clone.refs_2_), custom_call_target="tpu_custom_call" | custom-call | tf_op jit(solution)/shard_map/pallas_call | solution.py:240
  31.7 14.9 %all_to_all.11.refs_0_ = bf16[24,8,128]{2,1,0:T(8,128)(2,1)S(1)} all-to-all(bf16[24,8,128]{2,1,0:T(8,128)(2,1)S(1)} %shard_map.78), channel_id=1, replica_groups=mesh['energy'=24,'tile'=32] {'energy'}, dimensions={0} | all-to-all | bytes 98304 | tf_op jit(solution)/shard_map/all_to_all | solution.py:248
  46.6 0.0 copy-done.1
  46.6 0.1 shard_map.79
  46.8 4.7 %collective-permute-start = (bf16[32,512]{1,0:T(8,128)(2,1)S(1)}, bf16[32,512]{1,0:T(8,128)(2,1)S(1)}, u32[]{:S(2)}, u32[]{:S(2)}) collective-permute-start(bf16[32,512]{1,0:T(8,128)(2,1)S(1)} %get-tuple-element.11.own_ref), channel_id=1, source_target_pairs={{0,1},{1,0},{2,3},{3,2},{4,5},{5,4},{6,7},{7,6},{8,9},{9,8},{10,11... | collective-permute-start | bytes 98312 | tf_op jit(solution)/shard_map/ppermute | solution.py:279
  51.5 4.3 %collective-permute-start.1 = (bf16[32,512]{1,0:T(8,128)(2,1)S(1)}, bf16[32,512]{1,0:T(8,128)(2,1)S(1)}, u32[]{:S(2)}, u32[]{:S(2)}) collective-permute-start(bf16[32,512]{1,0:T(8,128)(2,1)S(1)} %get-tuple-element.11.own_ref), channel_id=1, source_target_pairs={{1,2},{2,1},{3,4},{4,3},{5,6},{6,5},{7,8},{8,7},{9,10},{10,9},{11,... | collective-permute-start | bytes 98312 | tf_op jit(solution)/shard_map/ppermute | solution.py:278
  55.9 0.0 collective-permute-done.chip_ref
  55.9 0.0 copy-done
  55.9 0.3 shard_map.81.refs_1_
  56.2 4.8 %collective-permute-done.1.refs_2_ = bf16[32,512]{1,0:T(8,128)(2,1)S(1)} collective-permute-done((bf16[32,512]{1,0:T(8,128)(2,1)S(1)}, bf16[32,512]{1,0:T(8,128)(2,1)S(1)}, u32[]{:S(2)}, u32[]{:S(2)}) %collective-permute-start.1) | collective-permute-done | bytes 32800 | tf_op jit(solution)/shard_map/ppermute | solution.py:278
  61.0 0.2 shard_map.82
  61.2 1.9 %collective-permute-start.2 = (bf16[32,512]{1,0:T(8,128)(2,1)S(1)}, bf16[32,512]{1,0:T(8,128)(2,1)S(1)}, u32[]{:S(2)}, u32[]{:S(2)}) collective-permute-start(bf16[32,512]{1,0:T(8,128)(2,1)S(1)} %get-tuple-element.12.own_ref), channel_id=1, source_target_pairs={{0,1},{1,0},{2,3},{3,2},{4,5},{5,4},{6,7},{7,6},{8,9},{9,8},{10,11... | collective-permute-start | bytes 98312 | tf_op jit(solution)/shard_map/ppermute | solution.py:279
  63.1 4.3 %collective-permute-start.3 = (bf16[32,512]{1,0:T(8,128)(2,1)S(1)}, bf16[32,512]{1,0:T(8,128)(2,1)S(1)}, u32[]{:S(2)}, u32[]{:S(2)}) collective-permute-start(bf16[32,512]{1,0:T(8,128)(2,1)S(1)} %get-tuple-element.12.own_ref), channel_id=1, source_target_pairs={{1,2},{2,1},{3,4},{4,3},{5,6},{6,5},{7,8},{8,7},{9,10},{10,9},{11,... | collective-permute-start | bytes 98312 | tf_op jit(solution)/shard_map/ppermute | solution.py:278
  67.5 0.7 shard_map.80
  68.1 0.0 collective-permute-done.2.chip_ref
  68.1 0.3 shard_map.83.refs_1_
  68.4 4.1 %collective-permute-done.3.refs_2_ = bf16[32,512]{1,0:T(8,128)(2,1)S(1)} collective-permute-done((bf16[32,512]{1,0:T(8,128)(2,1)S(1)}, bf16[32,512]{1,0:T(8,128)(2,1)S(1)}, u32[]{:S(2)}, u32[]{:S(2)}) %collective-permute-start.3) | collective-permute-done | bytes 32800 | tf_op jit(solution)/shard_map/ppermute | solution.py:278
  72.6 0.9 %shard_map.84 = f32[32,512]{1,0:T(8,128)} custom-call(s32[1]{0:T(128)} %bitcast.1.parity_ref.refs_0_, f32[32,512]{1,0:T(8,128)S(1)} %shard_map.83.refs_1_, bf16[32,512]{1,0:T(8,128)(2,1)S(1)} %collective-permute-done.3.refs_2_, f32[32,512]{1,0:T(8,128)S(1)} %get-tuple-element.10.sorted_ref.refs_3_.refs_4_, f32[32,512]{1,0:T(8,128)S(1)} %get-tuple-element.13.refs_4_, ...), custom_call_target="tpu_custom_call" | custom-call | tf_op jit(solution)/shard_map/pallas_call | solution.py:287
Async XLA Ops:
  2.4 44.2 %copy-start.1 = (f32[512]{0:T(512)S(1)}, f32[512]{0:T(512)}, u32[]{:S(2)}) copy-start(f32[512]{0:T(512)} %param.8) | copy-start | bytes 6148
  2.4 53.5 %copy-start = (bf16[3,512,512]{2,1,0:T(8,128)(2,1)S(1)}, bf16[3,512,512]{2,1,0:T(8,128)(2,1)}, u32[]{:S(2)}) copy-start(bf16[3,512,512]{2,1,0:T(8,128)(2,1)} %refs_6_.3) | copy-start | bytes 4718596
  46.8 9.1 %collective-permute-start = (bf16[32,512]{1,0:T(8,128)(2,1)S(1)}, bf16[32,512]{1,0:T(8,128)(2,1)S(1)}, u32[]{:S(2)}, u32[]{:S(2)}) collective-permute-start(bf16[32,512]{1,0:T(8,128)(2,1)S(1)} %get-tuple-element.11.own_ref), channel_id=1, source_target_pairs={{0,1},{1,0},{2,3},{3,2},{4,5},{5,4},{6,7},{7,6},{8,9},{9,8},{10,11... | collective-permute-start | bytes 98312 | tf_op jit(solution)/shard_map/ppermute | solution.py:279
  51.5 9.5 %collective-permute-start.1 = (bf16[32,512]{1,0:T(8,128)(2,1)S(1)}, bf16[32,512]{1,0:T(8,128)(2,1)S(1)}, u32[]{:S(2)}, u32[]{:S(2)}) collective-permute-start(bf16[32,512]{1,0:T(8,128)(2,1)S(1)} %get-tuple-element.11.own_ref), channel_id=1, source_target_pairs={{1,2},{2,1},{3,4},{4,3},{5,6},{6,5},{7,8},{8,7},{9,10},{10,9},{11,... | collective-permute-start | bytes 98312 | tf_op jit(solution)/shard_map/ppermute | solution.py:278
  61.2 6.9 %collective-permute-start.2 = (bf16[32,512]{1,0:T(8,128)(2,1)S(1)}, bf16[32,512]{1,0:T(8,128)(2,1)S(1)}, u32[]{:S(2)}, u32[]{:S(2)}) collective-permute-start(bf16[32,512]{1,0:T(8,128)(2,1)S(1)} %get-tuple-element.12.own_ref), channel_id=1, source_target_pairs={{0,1},{1,0},{2,3},{3,2},{4,5},{5,4},{6,7},{7,6},{8,9},{9,8},{10,11... | collective-permute-start | bytes 98312 | tf_op jit(solution)/shard_map/ppermute | solution.py:279
  63.1 9.5 %collective-permute-start.3 = (bf16[32,512]{1,0:T(8,128)(2,1)S(1)}, bf16[32,512]{1,0:T(8,128)(2,1)S(1)}, u32[]{:S(2)}, u32[]{:S(2)}) collective-permute-start(bf16[32,512]{1,0:T(8,128)(2,1)S(1)} %get-tuple-element.12.own_ref), channel_id=1, source_target_pairs={{1,2},{2,1},{3,4},{4,3},{5,6},{6,5},{7,8},{8,7},{9,10},{10,9},{11,... | collective-permute-start | bytes 98312 | tf_op jit(solution)/shard_map/ppermute | solution.py:278

commit v4 on v3

--- a/solution.py
+++ b/solution.py
@@ -16,18 +16,15 @@
 
 
 def dft_matrices(total):
-    half = total // 2
-    angle = 2.0 * np.pi / (2 * total)
-    freq = np.arange(half)[:, None]
-    rows = []
-    for parity in (0, 1):
-        at = 2 * np.arange(half)[None, :] + parity
-        cos = np.cos(angle * ((freq * at) % (2 * total)))
-        sin = np.sin(angle * ((freq * at) % (2 * total)))
-        edge = (half * at[0]) % (2 * total)
-        sin[0] = np.sin(angle * edge) if parity else np.cos(angle * edge)
-        rows.append(np.concatenate([cos, sin], axis=0))
-    return rows
+    rows, length = total // 4, 2 * total
+    freq = np.arange(rows)[:, None]
+    matrices = []
+    for r in range(4):
+        turn = (freq * (4 * np.arange(rows)[None, :] + r)) % length
+        cos, sin = np.cos(2.0 * np.pi * turn / length), np.sin(2.0 * np.pi * turn / length)
+        sin[0] = 1.0 - 2.0 * (np.arange(rows) % 2)
+        matrices.append(np.concatenate([cos, sin], axis=0))
+    return matrices
 
 
 def high_low(matrix):
@@ -37,21 +34,20 @@
     return high, low
 
 
-def pack_kernel(chunk, less_hbm, great_hbm, fwd_hbm, out_ref, fwd_ref, less_ref, great_ref, sems):
+def pack_kernel(chunk, less_hbm, great_hbm, fwd_hbm, back_hbm, out_ref, fwd_ref, back_ref, less_ref, great_ref, sems):
     copies = [
         pltpu.make_async_copy(src, dst, sems.at[n])
         for n, (src, dst) in enumerate(
-            ((less_hbm, less_ref), (great_hbm, great_ref), (fwd_hbm, fwd_ref))
+            ((less_hbm, less_ref), (great_hbm, great_ref), (fwd_hbm, fwd_ref), (back_hbm, back_ref))
         )
     ]
     for copy in copies:
         copy.start()
     e_dev, order = less_ref.shape[1], less_ref.shape[2]
-    half = e_dev // 2
     row = lax.broadcasted_iota(jnp.int32, (4 * e_dev, 4 * e_dev), 0)
     col = lax.broadcasted_iota(jnp.int32, (4 * e_dev, 4 * e_dev), 1)
     inner = row % e_dev
-    source = row - inner + jnp.where(inner < half, 2 * inner, 2 * (inner - half) + 1)
+    source = row - inner + 4 * (inner % 8) + inner // 8
     select = jnp.where(col == source, 1.0, 0.0).astype(jnp.bfloat16)
     lane = lax.broadcasted_iota(jnp.int32, (e_dev, LANES), 1)
     in_slot = lax.broadcasted_iota(jnp.int32, (8, LANES), 1) % SLOT
@@ -80,13 +76,16 @@
         ]
         out_ref[p] = jnp.concatenate(full, axis=0).astype(jnp.bfloat16)
     copies[2].wait()
-
-
-def correlate_kernel(chunk, scale, data_ref, fwd_ref, back_hbm, out_ref, back_ref, sem):
-    copy = pltpu.make_async_copy(back_hbm, back_ref, sem)
-    copy.start()
+    copies[3].wait()
+
+
+def product(a, b):
+    return a[0] * b[0] + a[1] * b[1], a[1] * b[0] - a[0] * b[1]
+
+
+def correlate_kernel(chunk, scale, data_ref, fwd_ref, back_ref, out_ref):
     blocks = data_ref.shape[0]
-    half = fwd_ref.shape[2] // 2
+    rows = back_ref.shape[1]
     in_slot = lax.broadcasted_iota(jnp.int32, (blocks, 8, LANES), 2) % SLOT
     spare = SLOT - chunk
     packed = [data_ref[:, 8 * g : 8 * (g + 1), :].astype(jnp.float32) for g in range(3)]
@@ -94,43 +93,56 @@
     for g in range(3):
         moved = pltpu.roll(packed[g], LANES - chunk + spare * g, 2)
         rest = moved if g == 0 else jnp.where(in_slot >= spare * g, moved, rest)
-    spec = []
-    for parity in (0, 1):
-        rows = packed[:2] if parity == 0 else [packed[2], rest]
-        rows = jnp.concatenate(rows, axis=1).reshape(half, LANES).astype(jnp.bfloat16)
-        rows = jnp.concatenate([rows, rows], axis=0)
-        full = jnp.dot(fwd_ref[parity], rows, preferred_element_type=jnp.float32)
-        spec.append((full[:half], full[half:]))
-    (ac_e, as_e), (ac_o, as_o) = spec
-    bc_e, bs_e, bc_o, bs_o = (pltpu.roll(x, LANES // 2, 1) for x in (ac_e, as_e, ac_o, as_o))
-    edge = lax.broadcasted_iota(jnp.int32, (half, LANES), 0) == 0
-    cc = ac_e * bc_e + ac_o * bc_o
-    ss = as_e * bs_e + as_o * bs_o
-    even_c = jnp.where(edge, 0.5 * cc, cc + ss)
-    even_s = jnp.where(edge, 0.5 * ss, as_e * bc_e + as_o * bc_o - ac_e * bs_e - ac_o * bs_o)
-    cc = ac_e * bc_o + ac_o * bc_e
-    odd_c = jnp.where(edge, 0.5 * cc, cc + as_e * bs_o + as_o * bs_e)
-    odd_s = jnp.where(
-        edge,
-        0.5 * (as_o * bs_e - as_e * bs_o),
-        as_e * bc_o + as_o * bc_e - ac_e * bs_o - ac_o * bs_e,
-    )
+    c, s = [], []
+    for r in range(4):
+        energies = (packed + [rest])[r].reshape(rows, LANES).astype(jnp.bfloat16)
+        full = jnp.dot(fwd_ref[r, :, :rows], energies, preferred_element_type=jnp.float32)
+        full = full + jnp.dot(fwd_ref[r, :, rows:], energies, preferred_element_type=jnp.float32)
+        c.append(full[:rows])
+        s.append(full[rows:])
+
+    def times_other(spectrum):
+        return product(spectrum, [pltpu.roll(x, LANES // 2, 1) for x in spectrum])
+
+    c02, c02m, c13, c13m = c[0] + c[2], c[0] - c[2], c[1] + c[3], c[1] - c[3]
+    s02, s02m, s13, s13m = s[0] + s[2], s[0] - s[2], s[1] + s[3], s[1] - s[3]
+    low, low_i = times_other((c02 + c13, s02 + s13))
+    top, top_i = times_other((c02 - c13, s13 - s02))
+    under, under_i = times_other((c02m + s13m, c13m - s02m))
+    over, over_i = times_other((c02m - s13m, c13m + s02m))
+    pairs = (
+        (low + top + under + over, low_i - top_i - under_i + over_i),
+        (low - top + under_i + over_i, low_i + top_i + under - over),
+        (low + top - under - over, low_i - top_i + under_i - over_i),
+        (low - top - under_i - over_i, low_i + top_i - under + over),
+    )
+    root = math.sqrt(0.5)
+    c0, z0 = [x[:8] for x in c], [x[:8] for x in s]
+    zero = jnp.zeros_like(c0[0])
+    first, _ = times_other((c0[0] + c0[1] + c0[2] + c0[3], zero))
+    final, _ = times_other((c0[0] - c0[1] + c0[2] - c0[3], zero))
+    mid, mid_i = times_other((c0[0] - c0[2], c0[1] - c0[3]))
+    turned_sum, turned_dif = root * (z0[1] + z0[3]), root * (z0[1] - z0[3])
+    quarter, quarter_i = times_other((z0[0] + turned_dif, turned_sum + z0[2]))
+    three, three_i = times_other((z0[0] - turned_dif, turned_sum - z0[2]))
+    edges = (
+        (0.5 * (first + final) + mid, quarter + three),
+        (0.5 * (first - final) + mid_i, root * (quarter - three + quarter_i + three_i)),
+        (0.5 * (first + final) - mid, quarter_i - three_i),
+        (0.5 * (first - final) - mid_i, root * (three - quarter + quarter_i + three_i)),
+    )
+    edge = lax.broadcasted_iota(jnp.int32, (8, LANES), 0) == 0
     lane = lax.broadcasted_iota(jnp.int32, (blocks, 8, LANES), 2)
     result = None
-    copy.wait()
-    for parity, (c, s) in enumerate(((even_c, even_s), (odd_c, odd_s))):
-        c = c - pltpu.roll(c, LANES - SLOT, 1)
-        s = s - pltpu.roll(s, LANES - SLOT, 1)
-        both = jnp.concatenate([c, s], axis=0).astype(jnp.bfloat16)
-        lags = jnp.dot(back_ref[parity], both, preferred_element_type=jnp.float32) * scale
-        lags = lags.reshape(blocks, 2, 8, LANES)
-        for g in (0, 1):
-            slot = 2 * parity + g
-            part = lags[:, g]
-            if slot == 0:
-                result = part
-            else:
-                result = jnp.where(lane >= SLOT * slot, pltpu.roll(part, SLOT * slot, 2), result)
+    for r in range(4):
+        both = []
+        for value, at_edge in zip(pairs[r], edges[r]):
+            value = jnp.concatenate([jnp.where(edge, at_edge, value[:8]), value[8:]], axis=0)
+            both.append(value - pltpu.roll(value, LANES - SLOT, 1))
+        both = jnp.concatenate(both, axis=0).astype(jnp.bfloat16)
+        lags = jnp.dot(back_ref[r], both, preferred_element_type=jnp.float32) * scale
+        lags = lags.reshape(blocks, 8, LANES)
+        result = lags if r == 0 else jnp.where(lane >= SLOT * r, pltpu.roll(lags, SLOT * r, 2), result)
     out_ref[...] = result.astype(out_ref.dtype)
 
 
@@ -142,12 +154,11 @@
 
 
 def store_in_order(sorted_rows, refs, at):
-    half = sorted_rows.shape[0] // 2
     for n in range(sorted_rows.shape[1] // LANES):
         lanes = slice(LANES * n, LANES * (n + 1))
         tile = at // LANES + n
-        refs[1][tile, pl.ds(0, half, stride=2), :] = sorted_rows[:half, lanes]
-        refs[1][tile, pl.ds(1, half, stride=2), :] = sorted_rows[half:, lanes]
+        for r in range(4):
+            refs[1][tile, pl.ds(r, 8, stride=4), :] = sorted_rows[8 * r : 8 * (r + 1), lanes]
         tile_copy(refs, tile).start()
 
 
@@ -224,25 +235,25 @@
     g_less, g_great, forward, backward = (
         pltpu.with_memory_space_constraint(x, pltpu.HBM) for x in (g_less, g_great, forward, backward)
     )
-    pieces, forward = pl.pallas_call(
+    pieces, forward, backward = pl.pallas_call(
         lambda *refs: pack_kernel(chunk, *refs),
         out_shape=(
             jax.ShapeDtypeStruct((n_energy, 24, LANES), jnp.bfloat16),
             jax.ShapeDtypeStruct(forward.shape, jnp.bfloat16),
+            jax.ShapeDtypeStruct(backward.shape, jnp.bfloat16),
         ),
-        in_specs=[hbm] * 3,
-        out_specs=(vmem,) * 2,
-        scratch_shapes=[pltpu.VMEM(g_less.shape, jnp.bfloat16)] * 2 + [pltpu.SemaphoreType.DMA((3,))],
+        in_specs=[hbm] * 4,
+        out_specs=(vmem,) * 3,
+        scratch_shapes=[pltpu.VMEM(g_less.shape, jnp.bfloat16)] * 2 + [pltpu.SemaphoreType.DMA((4,))],
         compiler_params=limit,
-    )(g_less, g_great, forward)
+    )(g_less, g_great, forward, backward)
     pieces = lax.all_to_all(pieces, "energy", 0, 0, tiled=True)
-    scale = 0.25 / math.sqrt(total) * 4.0 / (2 * total)
+    scale = 0.25 / math.sqrt(total) * 2.0 / (2 * total)
     lags = pl.pallas_call(
         lambda *refs: correlate_kernel(chunk, scale, *refs),
         out_shape=jax.ShapeDtypeStruct((n_energy, 8, LANES), jnp.bfloat16),
-        in_specs=[vmem, vmem, hbm],
+        in_specs=[vmem] * 3,
         out_specs=vmem,
-        scratch_shapes=[pltpu.VMEM(backward.shape, jnp.bfloat16), pltpu.SemaphoreType.DMA(())],
         compiler_params=limit,
     )(pieces, forward, backward)
     lags = lax.all_to_all(lags, "energy", 0, 0, tiled=True)

time: 73.8 us -> 72.2 us (0.978)
  Pallas kernels: 6.86 us -> 5.36 us
    pallas_call x1, Pallas kernels: 2.66 us -> 1.27 us  [per_device(): pl.pallas_call(lambda *refs: correlate_kernel(chunk, scale, *refs), out_s...]
where the time goes in v4:
time: 72.2 us; the launch traced here: 71.9 us
  blocking collectives  41.5 us (57%)
  starting transfers between devices  15.3 us (21%)
  waiting for transfers between devices  8.95 us (12%)
  Pallas kernels  5.36 us (7%)
  between operations  0.75 us (1%)
    all_to_all x1, blocking collectives, per_device(): pieces = lax.all_to_all(pieces, 'energy', 0, 0, tiled=True)  26.6 us
    all_to_all x1, blocking collectives, per_device(): lags = lax.all_to_all(lags, 'energy', 0, 0, tiled=True)  14.9 us
    ppermute x2, waiting for transfers between devices, per_device(): far = lax.ppermute(resid_b, 'tile', far_pairs)  8.94 us
    ppermute x2, starting transfers between devices, per_device(): far = lax.ppermute(resid_b, 'tile', far_pairs)  8.68 us
    ppermute x2, starting transfers between devices, per_device(): chip = lax.ppermute(resid_b, 'tile', chip_pairs)  6.64 us
    pallas_call x1, Pallas kernels, per_device(): pl.pallas_call(lambda *refs: pack_kernel(chunk, *refs), out_shape=(jax.Sh...  1.66 us
  transfers between devices with their start and end apart: 4, of which 2 were waited for; matrix products, arithmetic and copies ran while one was open for 0% of the time, Pallas kernels for 2%

profile of v4, /device:TPU:23, one launch (start us, length us, event | category | flops | bytes accessed | tf_op | source)
XLA Modules:
  0.0 71.9 jit_solution(6558546250942598124)
XLA Ops:
  0.6 1.7 %shard_map.77 = (bf16[24,24,128]{2,1,0:T(8,128)(2,1)S(1)}, bf16[4,384,384]{2,1,0:T(8,128)(2,1)S(1)}, bf16[4,192,384]{2,1,0:T(8,128)(2,1)S(1)}) custom-call(bf16[2,32,512]{2,1,0:T(8,128)(2,1)} %refs_0_.1, bf16[2,32,512]{2,1,0:T(8,128)(2,1)} %refs_1_.1, bf16[4,384,384]{2,1,0:T(8,128)(2,1)} %constant.21.clone.refs_2_, bf16[4,192,384]{2,1,0:T(8,128)(2,1)} %constant.22.clone.refs_3_), custom_call_target="tpu_custom_call" | custom-call | tf_op jit(solution)/shard_map/pallas_call | solution.py:238
  2.3 0.0 copy-start.1
  2.3 0.0 copy-start
  2.3 26.6 %all_to_all.10.refs_0_ = bf16[24,24,128]{2,1,0:T(8,128)(2,1)S(1)} all-to-all(bf16[24,24,128]{2,1,0:T(8,128)(2,1)S(1)} %get-tuple-element.9), channel_id=1, replica_groups=mesh['energy'=24,'tile'=32] {'energy'}, dimensions={0} | all-to-all | bytes 294912 | tf_op jit(solution)/shard_map/all_to_all | solution.py:250
  28.9 1.3 %shard_map.78 = bf16[24,8,128]{2,1,0:T(8,128)(2,1)S(1)} custom-call(bf16[24,24,128]{2,1,0:T(8,128)(2,1)S(1)} %all_to_all.10.refs_0_, bf16[4,384,384]{2,1,0:T(8,128)(2,1)S(1)} %get-tuple-element.10.refs_1_, bf16[4,192,384]{2,1,0:T(8,128)(2,1)S(1)} %get-tuple-element.11.refs_2_), custom_call_target="tpu_custom_call" | custom-call | tf_op jit(solution)/shard_map/pallas_call | solution.py:252
  30.2 14.9 %all_to_all.11.refs_0_ = bf16[24,8,128]{2,1,0:T(8,128)(2,1)S(1)} all-to-all(bf16[24,8,128]{2,1,0:T(8,128)(2,1)S(1)} %shard_map.78), channel_id=1, replica_groups=mesh['energy'=24,'tile'=32] {'energy'}, dimensions={0} | all-to-all | bytes 98304 | tf_op jit(solution)/shard_map/all_to_all | solution.py:259
  45.1 0.0 copy-done.1
  45.1 0.1 shard_map.79
  45.3 4.7 %collective-permute-start = (bf16[32,512]{1,0:T(8,128)(2,1)S(1)}, bf16[32,512]{1,0:T(8,128)(2,1)S(1)}, u32[]{:S(2)}, u32[]{:S(2)}) collective-permute-start(bf16[32,512]{1,0:T(8,128)(2,1)S(1)} %get-tuple-element.13.own_ref), channel_id=1, source_target_pairs={{0,1},{1,0},{2,3},{3,2},{4,5},{5,4},{6,7},{7,6},{8,9},{9,8},{10,11... | collective-permute-start | bytes 98312 | tf_op jit(solution)/shard_map/ppermute | solution.py:290
  50.0 4.3 %collective-permute-start.1 = (bf16[32,512]{1,0:T(8,128)(2,1)S(1)}, bf16[32,512]{1,0:T(8,128)(2,1)S(1)}, u32[]{:S(2)}, u32[]{:S(2)}) collective-permute-start(bf16[32,512]{1,0:T(8,128)(2,1)S(1)} %get-tuple-element.13.own_ref), channel_id=1, source_target_pairs={{1,2},{2,1},{3,4},{4,3},{5,6},{6,5},{7,8},{8,7},{9,10},{10,9},{11,... | collective-permute-start | bytes 98312 | tf_op jit(solution)/shard_map/ppermute | solution.py:289
  54.4 0.0 collective-permute-done.chip_ref
  54.4 0.0 copy-done
  54.4 0.3 shard_map.81.refs_1_
  54.7 4.8 %collective-permute-done.1.refs_2_ = bf16[32,512]{1,0:T(8,128)(2,1)S(1)} collective-permute-done((bf16[32,512]{1,0:T(8,128)(2,1)S(1)}, bf16[32,512]{1,0:T(8,128)(2,1)S(1)}, u32[]{:S(2)}, u32[]{:S(2)}) %collective-permute-start.1) | collective-permute-done | bytes 32800 | tf_op jit(solution)/shard_map/ppermute | solution.py:289
  59.5 0.2 shard_map.82
  59.7 1.9 %collective-permute-start.2 = (bf16[32,512]{1,0:T(8,128)(2,1)S(1)}, bf16[32,512]{1,0:T(8,128)(2,1)S(1)}, u32[]{:S(2)}, u32[]{:S(2)}) collective-permute-start(bf16[32,512]{1,0:T(8,128)(2,1)S(1)} %get-tuple-element.14.own_ref), channel_id=1, source_target_pairs={{0,1},{1,0},{2,3},{3,2},{4,5},{5,4},{6,7},{7,6},{8,9},{9,8},{10,11... | collective-permute-start | bytes 98312 | tf_op jit(solution)/shard_map/ppermute | solution.py:290
  61.6 4.3 %collective-permute-start.3 = (bf16[32,512]{1,0:T(8,128)(2,1)S(1)}, bf16[32,512]{1,0:T(8,128)(2,1)S(1)}, u32[]{:S(2)}, u32[]{:S(2)}) collective-permute-start(bf16[32,512]{1,0:T(8,128)(2,1)S(1)} %get-tuple-element.14.own_ref), channel_id=1, source_target_pairs={{1,2},{2,1},{3,4},{4,3},{5,6},{6,5},{7,8},{8,7},{9,10},{10,9},{11,... | collective-permute-start | bytes 98312 | tf_op jit(solution)/shard_map/ppermute | solution.py:289
  66.0 0.7 shard_map.80
  66.6 0.0 collective-permute-done.2.chip_ref
  66.7 0.3 shard_map.83.refs_1_
  66.9 4.1 %collective-permute-done.3.refs_2_ = bf16[32,512]{1,0:T(8,128)(2,1)S(1)} collective-permute-done((bf16[32,512]{1,0:T(8,128)(2,1)S(1)}, bf16[32,512]{1,0:T(8,128)(2,1)S(1)}, u32[]{:S(2)}, u32[]{:S(2)}) %collective-permute-start.3) | collective-permute-done | bytes 32800 | tf_op jit(solution)/shard_map/ppermute | solution.py:289
  71.1 0.9 %shard_map.84 = f32[32,512]{1,0:T(8,128)} custom-call(s32[1]{0:T(128)} %bitcast.1.parity_ref.refs_0_, f32[32,512]{1,0:T(8,128)S(1)} %shard_map.83.refs_1_, bf16[32,512]{1,0:T(8,128)(2,1)S(1)} %collective-permute-done.3.refs_2_, f32[32,512]{1,0:T(8,128)S(1)} %get-tuple-element.12.sorted_ref.refs_3_.refs_4_, f32[32,512]{1,0:T(8,128)S(1)} %get-tuple-element.15.refs_4_, ...), custom_call_target="tpu_custom_call" | custom-call | tf_op jit(solution)/shard_map/pallas_call | solution.py:298
Async XLA Ops:
  2.3 42.8 %copy-start.1 = (f32[512]{0:T(512)S(1)}, f32[512]{0:T(512)}, u32[]{:S(2)}) copy-start(f32[512]{0:T(512)} %param.8) | copy-start | bytes 6148
  2.3 52.1 %copy-start = (bf16[3,512,512]{2,1,0:T(8,128)(2,1)S(1)}, bf16[3,512,512]{2,1,0:T(8,128)(2,1)}, u32[]{:S(2)}) copy-start(bf16[3,512,512]{2,1,0:T(8,128)(2,1)} %refs_6_.3) | copy-start | bytes 4718596
  45.3 9.1 %collective-permute-start = (bf16[32,512]{1,0:T(8,128)(2,1)S(1)}, bf16[32,512]{1,0:T(8,128)(2,1)S(1)}, u32[]{:S(2)}, u32[]{:S(2)}) collective-permute-start(bf16[32,512]{1,0:T(8,128)(2,1)S(1)} %get-tuple-element.13.own_ref), channel_id=1, source_target_pairs={{0,1},{1,0},{2,3},{3,2},{4,5},{5,4},{6,7},{7,6},{8,9},{9,8},{10,11... | collective-permute-start | bytes 98312 | tf_op jit(solution)/shard_map/ppermute | solution.py:290
  50.0 9.5 %collective-permute-start.1 = (bf16[32,512]{1,0:T(8,128)(2,1)S(1)}, bf16[32,512]{1,0:T(8,128)(2,1)S(1)}, u32[]{:S(2)}, u32[]{:S(2)}) collective-permute-start(bf16[32,512]{1,0:T(8,128)(2,1)S(1)} %get-tuple-element.13.own_ref), channel_id=1, source_target_pairs={{1,2},{2,1},{3,4},{4,3},{5,6},{6,5},{7,8},{8,7},{9,10},{10,9},{11,... | collective-permute-start | bytes 98312 | tf_op jit(solution)/shard_map/ppermute | solution.py:289
  59.7 6.9 %collective-permute-start.2 = (bf16[32,512]{1,0:T(8,128)(2,1)S(1)}, bf16[32,512]{1,0:T(8,128)(2,1)S(1)}, u32[]{:S(2)}, u32[]{:S(2)}) collective-permute-start(bf16[32,512]{1,0:T(8,128)(2,1)S(1)} %get-tuple-element.14.own_ref), channel_id=1, source_target_pairs={{0,1},{1,0},{2,3},{3,2},{4,5},{5,4},{6,7},{7,6},{8,9},{9,8},{10,11... | collective-permute-start | bytes 98312 | tf_op jit(solution)/shard_map/ppermute | solution.py:290
  61.6 9.5 %collective-permute-start.3 = (bf16[32,512]{1,0:T(8,128)(2,1)S(1)}, bf16[32,512]{1,0:T(8,128)(2,1)S(1)}, u32[]{:S(2)}, u32[]{:S(2)}) collective-permute-start(bf16[32,512]{1,0:T(8,128)(2,1)S(1)} %get-tuple-element.14.own_ref), channel_id=1, source_target_pairs={{1,2},{2,1},{3,4},{4,3},{5,6},{6,5},{7,8},{8,7},{9,10},{10,9},{11,... | collective-permute-start | bytes 98312 | tf_op jit(solution)/shard_map/ppermute | solution.py:289

commit v5 on v4

--- a/solution.py
+++ b/solution.py
@@ -9,7 +9,7 @@
 from jax.experimental.pallas import tpu as pltpu
 from jax.sharding import PartitionSpec as P
 
-ITERS = 2
+EARLY = 4
 LANES = 128
 VMEM_BYTES = 16 * 1024 * 1024
 SLOT = 32
@@ -167,8 +167,8 @@
         tile_copy(refs, tile).wait()
 
 
-def unpack_kernel(chunk, data_ref, bare_ref, sorted_ref, resid_ref):
-    order = sorted_ref.shape[1]
+def unpack_kernel(chunk, data_ref, bare_ref, sorted_ref, message_ref):
+    e_dev, order = sorted_ref.shape
     lane = lax.broadcasted_iota(jnp.int32, (8, LANES), 1)
     for g in range(4):
         for tile in range(order // LANES):
@@ -180,8 +180,28 @@
                 value = moved if value is None else jnp.where(lane >= begin, moved, value)
                 p += 1
             sorted_ref[8 * g : 8 * (g + 1), LANES * tile : LANES * (tile + 1)] = value
-    bare = bare_ref[...]
-    resid_ref[...] = (bare * sorted_ref[...] * bare).astype(jnp.bfloat16)
+    message_ref[:e_dev] = sorted_ref[...].astype(jnp.bfloat16)
+    row = lax.broadcasted_iota(jnp.int32, (8, order), 0)
+    rest, lines = bare_ref[...], jnp.zeros((8, order), jnp.float32)
+    for n in range(3):
+        part = rest.astype(jnp.bfloat16).astype(jnp.float32)
+        lines = jnp.where(row == n, part, lines)
+        rest = rest - part
+    message_ref[e_dev:] = lines.astype(jnp.bfloat16)
+
+
+def opened(message_ref):
+    e_dev = message_ref.shape[0] - 8
+    polar = message_ref[:e_dev].astype(jnp.float32)
+    lines = message_ref[e_dev:].astype(jnp.float32)
+    bare = lines[0:1] + lines[1:2] + lines[2:3]
+    return polar, bare, bare * polar * bare
+
+
+def updated(polar, bare, resid, total):
+    corr = total.astype(jnp.bfloat16).astype(jnp.float32)
+    screened = bare + 0.5 * resid + corr
+    return screened, (bare - screened + bare * polar * screened).astype(jnp.bfloat16)
 
 
 def order_kernel(sorted_ref, *refs):
@@ -189,53 +209,45 @@
     wait_in_order(refs)
 
 
-def near_kernel(parity_ref, own_ref, chip_ref, precond_ref, out_ref):
-    which = 2 - parity_ref[0]
-    out_ref[...] = jnp.dot(own_ref[...], precond_ref[0], preferred_element_type=jnp.float32) + jnp.dot(
-        chip_ref[...], precond_ref[which], preferred_element_type=jnp.float32
-    )
-
-
-def step_kernel(last, parity_ref, near_ref, far_ref, polar_ref, screened_ref, bare_ref, precond_ref, *refs):
-    which = 1 + parity_ref[0]
-    far = far_ref[...]
-    width = 256 if last else far.shape[1]
+def times(rows, tile):
+    return jnp.dot(rows, tile, preferred_element_type=jnp.float32)
+
+
+def near_kernel(first, place_ref, own_ref, chip_ref, precond_ref, out_ref):
+    own, chip = (opened(x)[2].astype(jnp.bfloat16) if first else x[...] for x in (own_ref, chip_ref))
+    out_ref[...] = times(own, precond_ref[0]) + times(chip, precond_ref[2 - place_ref[0] % 2])
+
+
+def first_kernel(place_ref, near_ref, own_ref, far_ref, behind_ref, precond_ref, far_precond_ref, screened_ref, next_ref, far_next_ref):
+    odd = place_ref[0] % 2
+    polar, bare, resid = opened(own_ref)
+    far_polar, far_bare, far_resid = opened(far_ref)
+    behind = opened(behind_ref)[2].astype(jnp.bfloat16)
+    own, far = resid.astype(jnp.bfloat16), far_resid.astype(jnp.bfloat16)
+    total = near_ref[...] + times(far, precond_ref[1 + odd])
+    screened_ref[...], next_ref[...] = updated(polar, bare, resid, total)
+    total = times(far, far_precond_ref[0]) + times(behind, far_precond_ref[1 + odd]) + times(own, far_precond_ref[2 - odd])
+    far_next_ref[...] = updated(far_polar, far_bare, far_resid, total)[1]
+
+
+def last_kernel(place_ref, near_ref, far_ref, far_next_ref, polar_ref, screened_ref, bare_ref, precond_ref, *refs):
+    which = 1 + place_ref[0] % 2
+    far = jnp.where(place_ref[0] >= 2, far_next_ref[...], far_ref[...])
+    width = 256
     for at in range(0, far.shape[1], width):
         lanes = slice(at, at + width)
-        bare, polar = bare_ref[:, lanes], polar_ref[:, lanes]
-        screened = screened_ref[:, lanes] if last else jnp.broadcast_to(bare, polar.shape)
+        bare, polar, screened = bare_ref[:, lanes], polar_ref[:, lanes], screened_ref[:, lanes]
         resid = bare - screened + bare * polar * screened
-        product = near_ref[:, lanes] + jnp.dot(far, precond_ref[which, :, lanes], preferred_element_type=jnp.float32)
-        corr = product.astype(jnp.bfloat16).astype(jnp.float32)
-        screened = screened + 0.5 * resid + corr
-        if last:
-            store_in_order(screened, refs, at)
-        else:
-            refs[0][:, lanes] = screened
-            refs[1][:, lanes] = (bare - screened + bare * polar * screened).astype(jnp.bfloat16)
-    if last:
-        wait_in_order(refs)
-
-
-def per_device(g_less, g_great, coulomb, precond):
-    e_dev, order = g_less.shape[1:]
-    n_energy = lax.axis_size("energy")
-    n_tile = lax.axis_size("tile")
-    total = e_dev * n_energy
-    chunk = -(-order // n_energy)
+        total = near_ref[:, lanes] + times(far, precond_ref[which, :, lanes])
+        corr = total.astype(jnp.bfloat16).astype(jnp.float32)
+        store_in_order(screened + 0.5 * resid + corr, refs, at)
+    wait_in_order(refs)
+
+
+def pack_call(chunk, n_energy, limit, g_less, g_great, forward, backward):
     vmem = pl.BlockSpec(memory_space=pltpu.VMEM)
-    smem = pl.BlockSpec(memory_space=pltpu.SMEM)
-
-    limit = pltpu.CompilerParams(vmem_limit_bytes=VMEM_BYTES)
-    matrices = [high_low(m) for m in dft_matrices(total)]
-    forward = jnp.asarray(np.stack([np.concatenate(pair, axis=1) for pair in matrices]))
-    backward = jnp.asarray(np.stack([np.ascontiguousarray(high.T) for high, _ in matrices]))
-
     hbm = pl.BlockSpec(memory_space=pltpu.HBM)
-    g_less, g_great, forward, backward = (
-        pltpu.with_memory_space_constraint(x, pltpu.HBM) for x in (g_less, g_great, forward, backward)
-    )
-    pieces, forward, backward = pl.pallas_call(
+    return pl.pallas_call(
         lambda *refs: pack_kernel(chunk, *refs),
         out_shape=(
             jax.ShapeDtypeStruct((n_energy, 24, LANES), jnp.bfloat16),
@@ -247,6 +259,37 @@
         scratch_shapes=[pltpu.VMEM(g_less.shape, jnp.bfloat16)] * 2 + [pltpu.SemaphoreType.DMA((4,))],
         compiler_params=limit,
     )(g_less, g_great, forward, backward)
+
+
+def per_device(g_less, g_great, coulomb, precond):
+    e_dev, order = g_less.shape[1:]
+    n_energy = lax.axis_size("energy")
+    n_tile = lax.axis_size("tile")
+    total = e_dev * n_energy
+    chunk = -(-order // n_energy)
+    vmem = pl.BlockSpec(memory_space=pltpu.VMEM)
+    smem = pl.BlockSpec(memory_space=pltpu.SMEM)
+
+    limit = pltpu.CompilerParams(vmem_limit_bytes=VMEM_BYTES)
+    matrices = [high_low(m) for m in dft_matrices(total)]
+    forward = jnp.asarray(np.stack([np.concatenate(pair, axis=1) for pair in matrices]))
+    backward = jnp.asarray(np.stack([np.ascontiguousarray(high.T) for high, _ in matrices]))
+
+    hbm = pl.BlockSpec(memory_space=pltpu.HBM)
+    g_less, g_great, forward, backward = (
+        pltpu.with_memory_space_constraint(x, pltpu.HBM) for x in (g_less, g_great, forward, backward)
+    )
+    block = [(i, i + 1 if i % 2 else i - 1) for i in range(1, n_tile - 1)]
+    ahead = [(i, i + 2 if i % 2 == 0 else i - 2) for i in range(n_tile) if 0 <= (i + 2 if i % 2 == 0 else i - 2) < n_tile]
+    early = [e % (n_energy // 2) < EARLY for e in range(n_energy)]
+
+    def pairs_of(pairs, chosen):
+        return [(e * n_tile + i, e * n_tile + j) for e in range(n_energy) if chosen[e] for i, j in pairs]
+
+    far_precond = lax.ppermute(precond, ("energy", "tile"), pairs_of(block, early))
+    pieces, forward, backward = pack_call(
+        chunk, n_energy, limit, g_less, g_great, forward, backward
+    )
     pieces = lax.all_to_all(pieces, "energy", 0, 0, tiled=True)
     scale = 0.25 / math.sqrt(total) * 2.0 / (2 * total)
     lags = pl.pallas_call(
@@ -264,9 +307,9 @@
         pltpu.VMEM((order // LANES, e_dev, LANES), jnp.float32),
         pltpu.SemaphoreType.DMA((order // LANES,)),
     ]
-    polar_sorted, resid_b = pl.pallas_call(
+    polar_sorted, message = pl.pallas_call(
         lambda *refs: unpack_kernel(chunk, *refs),
-        out_shape=(plane, plane_b),
+        out_shape=(plane, jax.ShapeDtypeStruct((e_dev + 8, order), jnp.bfloat16)),
         in_specs=[vmem] * 2,
         out_specs=(vmem,) * 2,
         compiler_params=limit,
@@ -280,31 +323,41 @@
         compiler_params=limit,
         cost_estimate=pl.CostEstimate(flops=1000, bytes_accessed=1000, transcendentals=0),
     )(polar_sorted)
-    parity = (lax.axis_index("tile") % 2).astype(jnp.int32).reshape(1)
-    screened = polar_sorted
+    is_early = (lax.axis_index("energy") % (n_energy // 2) < EARLY).astype(jnp.int32)
+    place = (lax.axis_index("tile") % 2 + 2 * is_early).astype(jnp.int32).reshape(1)
     chip_pairs = [(i, i ^ 1) for i in range(n_tile)]
-    far_pairs = [(i, i + 1 if i % 2 else i - 1) for i in range(1, n_tile - 1)]
-    for step in range(ITERS):
-        last = step == ITERS - 1
-        far = lax.ppermute(resid_b, "tile", far_pairs)
-        chip = lax.ppermute(resid_b, "tile", chip_pairs)
-        near = pl.pallas_call(
-            near_kernel,
+
+    def near_call(first, own, chip):
+        return pl.pallas_call(
+            lambda *refs: near_kernel(first, *refs),
             out_shape=plane,
             in_specs=[smem] + [vmem] * 3,
             out_specs=vmem,
             compiler_params=limit,
-        )(parity, resid_b, chip, precond)
-        out = pl.pallas_call(
-            lambda *refs, last=last: step_kernel(last, *refs),
-            out_shape=(plane,) if last else (plane, plane_b),
-            in_specs=[smem] + [vmem] * 6,
-            out_specs=(hbm,) if last else (vmem, vmem),
-            scratch_shapes=in_order if last else [],
-            compiler_params=limit,
-        )(parity, near, far, polar_sorted, screened, bare, precond)
-        screened = out[0]
-        resid_b = out[-1]
+        )(place, own, chip, precond)
+
+    behind = lax.ppermute(message, ("energy", "tile"), pairs_of(ahead, early))
+    far = lax.ppermute(message, "tile", block)
+    chip = lax.ppermute(message, "tile", chip_pairs)
+    near = near_call(True, message, chip)
+    screened, resid_b, far_b = pl.pallas_call(
+        first_kernel,
+        out_shape=(plane, plane_b, plane_b),
+        in_specs=[smem] + [vmem] * 6,
+        out_specs=(vmem,) * 3,
+        compiler_params=limit,
+    )(place, near, message, far, behind, precond, far_precond)
+    far = lax.ppermute(resid_b, ("energy", "tile"), pairs_of(block, [not e for e in early]))
+    chip = lax.ppermute(resid_b, "tile", chip_pairs)
+    near = near_call(False, resid_b, chip)
+    screened = pl.pallas_call(
+        last_kernel,
+        out_shape=plane,
+        in_specs=[smem] + [vmem] * 7,
+        out_specs=hbm,
+        scratch_shapes=in_order,
+        compiler_params=limit,
+    )(place, near, far, far_b, polar_sorted, screened, bare, precond)
     return (polar, screened)
 
 

time: 72.2 us -> 85 us (1.18)
  blocking collectives: 41.5 us -> 52.8 us
  starting transfers between devices: 15.3 us -> 18.7 us
  waiting for transfers between devices: 8.95 us -> 6.72 us
    ppermute x2 -> x5, starting transfers between devices: 8.68 us -> 16.8 us  [the longest x1 6.38 us: per_device(): far = lax.ppermute(message, 'tile', block)]
    all_to_all x1, blocking collectives: 26.6 us -> 34.4 us  [per_device(): pieces = lax.all_to_all(pieces, 'energy', 0, 0, tiled=True)]
    ppermute x2 -> x1, starting transfers between devices: 6.64 us -> 1.92 us  [per_device(): chip = lax.ppermute(resid_b, 'tile', chip_pairs)]
    all_to_all x1, blocking collectives: 14.9 us -> 18.3 us  [per_device(): lags = lax.all_to_all(lags, 'energy', 0, 0, tiled=True)]
    ppermute x2 -> x5, waiting for transfers between devices: 8.94 us -> 6.72 us  [the longest x1 5.81 us: per_device(): behind = lax.ppermute(message, ('energy', 'tile'), pairs_of(ahead, early))]
  transfers between devices with their start and end apart: 4 -> 6, of which waited for: 2 -> 2; matrix products, arithmetic and copies ran while one was open for 0% -> 0% of each run, Pallas kernels for 2% -> 5%
where the time goes in v5:
time: 85 us; the launch traced here: 84.7 us
  blocking collectives  52.8 us (62%)
  starting transfers between devices  18.7 us (22%)
  waiting for transfers between devices  6.72 us (8%)
  Pallas kernels  5.67 us (7%)
    all_to_all x1, blocking collectives, per_device(): pieces = lax.all_to_all(pieces, 'energy', 0, 0, tiled=True)  34.4 us
    all_to_all x1, blocking collectives, per_device(): lags = lax.all_to_all(lags, 'energy', 0, 0, tiled=True)  18.3 us
    ppermute x1, starting transfers between devices, per_device(): far = lax.ppermute(message, 'tile', block)  6.38 us
    ppermute x1, starting transfers between devices, per_device(): lax.ppermute(precond, ('energy', 'tile'), pairs_of(block, early))  5.91 us
    ppermute x1, waiting for transfers between devices, per_device(): behind = lax.ppermute(message, ('energy', 'tile'), pairs_of(ahead, early))  5.81 us
    ppermute x1, starting transfers between devices, per_device(): chip = lax.ppermute(message, 'tile', chip_pairs)  1.92 us
    ppermute x1, starting transfers between devices, per_device(): behind = lax.ppermute(message, ('energy', 'tile'), pairs_of(ahead, early))  1.92 us
    ppermute x1, starting transfers between devices, per_device(): chip = lax.ppermute(resid_b, 'tile', chip_pairs)  1.92 us
  transfers between devices with their start and end apart: 6, of which 2 were waited for; matrix products, arithmetic and copies ran while one was open for 0% of the time, Pallas kernels for 5%

profile of v5, /device:TPU:23, one launch (start us, length us, event | category | flops | bytes accessed | tf_op | source)
XLA Modules:
  0.0 84.7 jit_solution(3401261138601980105)
XLA Ops:
  0.6 5.9 %collective-permute-start.3 = (bf16[3,512,512]{2,1,0:T(8,128)(2,1)}, bf16[3,512,512]{2,1,0:T(8,128)(2,1)S(1)}, u32[]{:S(2)}, u32[]{:S(2)}) collective-permute-start(bf16[3,512,512]{2,1,0:T(8,128)(2,1)} %precond_ref.3), channel_id=1, source_target_pairs={{1,2},{2,1},{3,4},{4,3},{5,6},{6,5},{7,8},{8,7},{9,10},{10,9},{11,... | collective-permute-start | bytes 4718600 | tf_op jit(solution)/shard_map/ppermute | solution.py:289
  6.5 1.7 %shard_map.77 = (bf16[24,24,128]{2,1,0:T(8,128)(2,1)S(1)}, bf16[4,384,384]{2,1,0:T(8,128)(2,1)S(1)}, bf16[4,192,384]{2,1,0:T(8,128)(2,1)S(1)}) custom-call(bf16[2,32,512]{2,1,0:T(8,128)(2,1)} %refs_0_.1, bf16[2,32,512]{2,1,0:T(8,128)(2,1)} %refs_1_.1, bf16[4,384,384]{2,1,0:T(8,128)(2,1)} %constant.35.clone.refs_2_, bf16[4,192,384]{2,1,0:T(8,128)(2,1)} %constant.36.clone.refs_3_), custom_call_target="tpu_custom_call" | custom-call | tf_op jit(solution)/shard_map/pallas_call | solution.py:250
  8.2 0.0 copy-start.1
  8.2 0.0 copy-start
  8.2 34.4 %all_to_all.10.refs_0_ = bf16[24,24,128]{2,1,0:T(8,128)(2,1)S(1)} all-to-all(bf16[24,24,128]{2,1,0:T(8,128)(2,1)S(1)} %get-tuple-element.10), channel_id=1, replica_groups=mesh['energy'=24,'tile'=32] {'energy'}, dimensions={0} | all-to-all | bytes 294912 | tf_op jit(solution)/shard_map/all_to_all | solution.py:293
  42.7 1.3 %shard_map.78 = bf16[24,8,128]{2,1,0:T(8,128)(2,1)S(1)} custom-call(bf16[24,24,128]{2,1,0:T(8,128)(2,1)S(1)} %all_to_all.10.refs_0_, bf16[4,384,384]{2,1,0:T(8,128)(2,1)S(1)} %get-tuple-element.11.refs_1_, bf16[4,192,384]{2,1,0:T(8,128)(2,1)S(1)} %get-tuple-element.12.refs_2_), custom_call_target="tpu_custom_call" | custom-call | tf_op jit(solution)/shard_map/pallas_call | solution.py:295
  44.0 18.3 %all_to_all.11.refs_0_ = bf16[24,8,128]{2,1,0:T(8,128)(2,1)S(1)} all-to-all(bf16[24,8,128]{2,1,0:T(8,128)(2,1)S(1)} %shard_map.78), channel_id=1, replica_groups=mesh['energy'=24,'tile'=32] {'energy'}, dimensions={0} | all-to-all | bytes 98304 | tf_op jit(solution)/shard_map/all_to_all | solution.py:302
  62.3 0.1 shard_map.79
  62.5 1.9 %collective-permute-start = (bf16[40,512]{1,0:T(8,128)(2,1)S(1)}, bf16[40,512]{1,0:T(8,128)(2,1)S(1)}, u32[]{:S(2)}, u32[]{:S(2)}) collective-permute-start(bf16[40,512]{1,0:T(8,128)(2,1)S(1)} %get-tuple-element.14.refs_1_.own_ref), channel_id=1, source_target_pairs={{0,1},{1,0},{2,3},{3,2},{4,5},{5,4},{6,7},{7,6},{8,9},{9,8},{10,11... | collective-permute-start | bytes 122888 | tf_op jit(solution)/shard_map/ppermute | solution.py:341
  64.4 6.4 %collective-permute-start.1 = (bf16[40,512]{1,0:T(8,128)(2,1)S(1)}, bf16[40,512]{1,0:T(8,128)(2,1)S(1)}, u32[]{:S(2)}, u32[]{:S(2)}) collective-permute-start(bf16[40,512]{1,0:T(8,128)(2,1)S(1)} %get-tuple-element.14.refs_1_.own_ref), channel_id=1, source_target_pairs={{1,2},{2,1},{3,4},{4,3},{5,6},{6,5},{7,8},{8,7},{9,10},{10,9},{11,... | collective-permute-start | bytes 122888 | tf_op jit(solution)/shard_map/ppermute | solution.py:340
  70.8 1.9 %collective-permute-start.2 = (bf16[40,512]{1,0:T(8,128)(2,1)S(1)}, bf16[40,512]{1,0:T(8,128)(2,1)S(1)}, u32[]{:S(2)}, u32[]{:S(2)}) collective-permute-start(bf16[40,512]{1,0:T(8,128)(2,1)S(1)} %get-tuple-element.14.refs_1_.own_ref), channel_id=1, source_target_pairs={{0,2},{2,4},{3,1},{4,6},{5,3},{6,8},{7,5},{8,10},{9,7},{10,12},{11... | collective-permute-start | bytes 122888 | tf_op jit(solution)/shard_map/ppermute | solution.py:339
  72.7 0.0 collective-permute-done.refs_2_
  72.7 0.3 shard_map.81.near_ref
  73.0 0.9 %collective-permute-done.1.far_ref = bf16[40,512]{1,0:T(8,128)(2,1)S(1)} collective-permute-done((bf16[40,512]{1,0:T(8,128)(2,1)S(1)}, bf16[40,512]{1,0:T(8,128)(2,1)S(1)}, u32[]{:S(2)}, u32[]{:S(2)}) %collective-permute-start.1) | collective-permute-done | bytes 40992 | tf_op jit(solution)/shard_map/ppermute | solution.py:340
  73.9 5.8 %collective-permute-done.2.behind_ref = bf16[40,512]{1,0:T(8,128)(2,1)S(1)} collective-permute-done((bf16[40,512]{1,0:T(8,128)(2,1)S(1)}, bf16[40,512]{1,0:T(8,128)(2,1)S(1)}, u32[]{:S(2)}, u32[]{:S(2)}) %collective-permute-start.2) | collective-permute-done | bytes 40992 | tf_op jit(solution)/shard_map/ppermute | solution.py:339
  79.7 0.0 collective-permute-done.3.far_precond_ref
  79.7 0.5 shard_map.82
  80.2 1.9 %collective-permute-start.4 = (bf16[32,512]{1,0:T(8,128)(2,1)S(1)}, bf16[32,512]{1,0:T(8,128)(2,1)S(1)}, u32[]{:S(2)}, u32[]{:S(2)}) collective-permute-start(bf16[32,512]{1,0:T(8,128)(2,1)S(1)} %get-tuple-element.15.refs_1_), channel_id=1, source_target_pairs={{0,1},{1,0},{2,3},{3,2},{4,5},{5,4},{6,7},{7,6},{8,9},{9,8},{10,11... | collective-permute-start | bytes 98312 | tf_op jit(solution)/shard_map/ppermute | solution.py:351
  82.2 0.7 collective-permute-start.5
  82.8 0.7 shard_map.80
  83.5 0.0 collective-permute-done.4.refs_2_
  83.5 0.3 shard_map.83.near_ref
  83.8 0.0 collective-permute-done.5.far_ref
  83.8 0.9 %shard_map.84 = f32[32,512]{1,0:T(8,128)} custom-call(s32[1]{0:T(128)} %bitcast.1.refs_0_.place_ref, f32[32,512]{1,0:T(8,128)S(1)} %shard_map.83.near_ref, bf16[32,512]{1,0:T(8,128)(2,1)S(1)} %collective-permute-done.5.far_ref, bf16[32,512]{1,0:T(8,128)(2,1)S(1)} %get-tuple-element.16.far_next_ref, f32[32,512]{1,0:T(8,128)S(1)} %get-tuple-element.13.sorted_ref.polar_ref, ...), custom_call_target="tpu_custom_call" | custom-call | tf_op jit(solution)/shard_map/pallas_call | solution.py:353
  (2 shorter events, 0.0 us)
Async XLA Ops:
  0.6 79.1 %collective-permute-start.3 = (bf16[3,512,512]{2,1,0:T(8,128)(2,1)}, bf16[3,512,512]{2,1,0:T(8,128)(2,1)S(1)}, u32[]{:S(2)}, u32[]{:S(2)}) collective-permute-start(bf16[3,512,512]{2,1,0:T(8,128)(2,1)} %precond_ref.3), channel_id=1, source_target_pairs={{1,2},{2,1},{3,4},{4,3},{5,6},{6,5},{7,8},{8,7},{9,10},{10,9},{11,... | collective-permute-start | bytes 4718600 | tf_op jit(solution)/shard_map/ppermute | solution.py:289
  8.2 54.1 %copy-start.1 = (f32[512]{0:T(512)S(1)}, f32[512]{0:T(512)}, u32[]{:S(2)}) copy-start(f32[512]{0:T(512)} %param.8) | copy-start | bytes 6148
  8.2 64.5 %copy-start = (bf16[3,512,512]{2,1,0:T(8,128)(2,1)S(1)}, bf16[3,512,512]{2,1,0:T(8,128)(2,1)}, u32[]{:S(2)}) copy-start(bf16[3,512,512]{2,1,0:T(8,128)(2,1)} %precond_ref.3) | copy-start | bytes 4718596
  62.5 10.3 %collective-permute-start = (bf16[40,512]{1,0:T(8,128)(2,1)S(1)}, bf16[40,512]{1,0:T(8,128)(2,1)S(1)}, u32[]{:S(2)}, u32[]{:S(2)}) collective-permute-start(bf16[40,512]{1,0:T(8,128)(2,1)S(1)} %get-tuple-element.14.refs_1_.own_ref), channel_id=1, source_target_pairs={{0,1},{1,0},{2,3},{3,2},{4,5},{5,4},{6,7},{7,6},{8,9},{9,8},{10,11... | collective-permute-start | bytes 122888 | tf_op jit(solution)/shard_map/ppermute | solution.py:341
  64.4 9.6 %collective-permute-start.1 = (bf16[40,512]{1,0:T(8,128)(2,1)S(1)}, bf16[40,512]{1,0:T(8,128)(2,1)S(1)}, u32[]{:S(2)}, u32[]{:S(2)}) collective-permute-start(bf16[40,512]{1,0:T(8,128)(2,1)S(1)} %get-tuple-element.14.refs_1_.own_ref), channel_id=1, source_target_pairs={{1,2},{2,1},{3,4},{4,3},{5,6},{6,5},{7,8},{8,7},{9,10},{10,9},{11,... | collective-permute-start | bytes 122888 | tf_op jit(solution)/shard_map/ppermute | solution.py:340
  70.8 9.0 %collective-permute-start.2 = (bf16[40,512]{1,0:T(8,128)(2,1)S(1)}, bf16[40,512]{1,0:T(8,128)(2,1)S(1)}, u32[]{:S(2)}, u32[]{:S(2)}) collective-permute-start(bf16[40,512]{1,0:T(8,128)(2,1)S(1)} %get-tuple-element.14.refs_1_.own_ref), channel_id=1, source_target_pairs={{0,2},{2,4},{3,1},{4,6},{5,3},{6,8},{7,5},{8,10},{9,7},{10,12},{11... | collective-permute-start | bytes 122888 | tf_op jit(solution)/shard_map/ppermute | solution.py:339
  80.2 3.3 %collective-permute-start.4 = (bf16[32,512]{1,0:T(8,128)(2,1)S(1)}, bf16[32,512]{1,0:T(8,128)(2,1)S(1)}, u32[]{:S(2)}, u32[]{:S(2)}) collective-permute-start(bf16[32,512]{1,0:T(8,128)(2,1)S(1)} %get-tuple-element.15.refs_1_), channel_id=1, source_target_pairs={{0,1},{1,0},{2,3},{3,2},{4,5},{5,4},{6,7},{7,6},{8,9},{9,8},{10,11... | collective-permute-start | bytes 98312 | tf_op jit(solution)/shard_map/ppermute | solution.py:351
  82.2 1.6 %collective-permute-start.5 = (bf16[32,512]{1,0:T(8,128)(2,1)S(1)}, bf16[32,512]{1,0:T(8,128)(2,1)S(1)}, u32[]{:S(2)}, u32[]{:S(2)}) collective-permute-start(bf16[32,512]{1,0:T(8,128)(2,1)S(1)} %get-tuple-element.15.refs_1_), channel_id=1, source_target_pairs={{129,130},{130,129},{131,132},{132,131},{133,134},{134,133},{135,1... | collective-permute-start | bytes 98312 | tf_op jit(solution)/shard_map/ppermute | solution.py:350

commit v6 on v4

--- a/solution.py
+++ b/solution.py
@@ -49,32 +49,41 @@
     inner = row % e_dev
     source = row - inner + 4 * (inner % 8) + inner // 8
     select = jnp.where(col == source, 1.0, 0.0).astype(jnp.bfloat16)
-    lane = lax.broadcasted_iota(jnp.int32, (e_dev, LANES), 1)
-    in_slot = lax.broadcasted_iota(jnp.int32, (8, LANES), 1) % SLOT
+    lane = lax.broadcasted_iota(jnp.int32, (8, LANES), 1)
     spare = SLOT - chunk
     copies[0].wait()
     copies[1].wait()
     rows = jnp.concatenate([less_ref[0], less_ref[1], great_ref[0], great_ref[1]], axis=0)
     sorted_rows = jnp.dot(select, rows, preferred_element_type=jnp.float32)
+
+    def moved(q, r, tile, shift):
+        part = sorted_rows[e_dev * q + 8 * r : e_dev * q + 8 * (r + 1), LANES * tile : LANES * (tile + 1)]
+        return pltpu.roll(part, shift % LANES, 1) if shift % LANES else part
+
+    tiles = range(order // LANES)
+    main = [[[moved(q, g, t, SLOT * q) for t in tiles] for g in range(3)] for q in range(4)]
+    rest = [[[moved(q, 3, t, SLOT * q + chunk - spare * g) for t in tiles] for g in range(3)] for q in range(4)]
     for p in range(out_ref.shape[0]):
         low = chunk * p
-        high = min(low + chunk, order) - 1
-        first, last = low // LANES, high // LANES
-        piece = None
-        for q in range(4):
-            shift = (SLOT * q - low) % LANES
-            part = sorted_rows[e_dev * q : e_dev * (q + 1)]
-            moved = pltpu.roll(part[:, LANES * first : LANES * (first + 1)], shift, 1)
+        first, last = low // LANES, (min(low + chunk, order) - 1) // LANES
+        turn = low % LANES
+        place = (lane - turn) & (LANES - 1)
+        inner = place & (SLOT - 1)
+
+        def chain(parts, g, tile):
+            value = parts[0][g][tile]
+            for q in range(1, 4):
+                value = jnp.where(place >= SLOT * q, parts[q][g][tile], value)
+            return value
+
+        groups = []
+        for g in range(3):
+            ours, extra = chain(main, g, first), chain(rest, g, first)
             if last > first:
-                after = pltpu.roll(part[:, LANES * last : LANES * (last + 1)], shift, 1)
-                moved = jnp.where(lane >= SLOT * q + LANES * last - low, after, moved)
-            piece = moved if q == 0 else jnp.where(lane >= SLOT * q, moved, piece)
-        rest = piece[24:]
-        full = [
-            jnp.where(in_slot < chunk, piece[8 * g : 8 * (g + 1)], pltpu.roll(rest, chunk - spare * g, 1))
-            for g in range(3)
-        ]
-        out_ref[p] = jnp.concatenate(full, axis=0).astype(jnp.bfloat16)
+                ours = jnp.where(inner >= LANES - turn, chain(main, g, last), ours)
+                extra = jnp.where(inner - chunk + spare * g >= LANES - turn, chain(rest, g, last), extra)
+            groups.append(jnp.where(inner < chunk, ours, extra))
+        out_ref[p] = jnp.concatenate(groups, axis=0).astype(jnp.bfloat16)
     copies[2].wait()
     copies[3].wait()
 
@@ -86,7 +95,9 @@
 def correlate_kernel(chunk, scale, data_ref, fwd_ref, back_ref, out_ref):
     blocks = data_ref.shape[0]
     rows = back_ref.shape[1]
-    in_slot = lax.broadcasted_iota(jnp.int32, (blocks, 8, LANES), 2) % SLOT
+    turn = chunk * lax.axis_index("energy")
+    place = (lax.broadcasted_iota(jnp.int32, (blocks, 8, LANES), 2) - turn) & (LANES - 1)
+    in_slot = place & (SLOT - 1)
     spare = SLOT - chunk
     packed = [data_ref[:, 8 * g : 8 * (g + 1), :].astype(jnp.float32) for g in range(3)]
     rest = None
@@ -97,7 +108,6 @@
     for r in range(4):
         energies = (packed + [rest])[r].reshape(rows, LANES).astype(jnp.bfloat16)
         full = jnp.dot(fwd_ref[r, :, :rows], energies, preferred_element_type=jnp.float32)
-        full = full + jnp.dot(fwd_ref[r, :, rows:], energies, preferred_element_type=jnp.float32)
         c.append(full[:rows])
         s.append(full[rows:])
 
@@ -132,7 +142,6 @@
         (0.5 * (first - final) - mid_i, root * (three - quarter + quarter_i + three_i)),
     )
     edge = lax.broadcasted_iota(jnp.int32, (8, LANES), 0) == 0
-    lane = lax.broadcasted_iota(jnp.int32, (blocks, 8, LANES), 2)
     result = None
     for r in range(4):
         both = []
@@ -142,7 +151,7 @@
         both = jnp.concatenate(both, axis=0).astype(jnp.bfloat16)
         lags = jnp.dot(back_ref[r], both, preferred_element_type=jnp.float32) * scale
         lags = lags.reshape(blocks, 8, LANES)
-        result = lags if r == 0 else jnp.where(lane >= SLOT * r, pltpu.roll(lags, SLOT * r, 2), result)
+        result = lags if r == 0 else jnp.where(place >= SLOT * r, pltpu.roll(lags, SLOT * r, 2), result)
     out_ref[...] = result.astype(out_ref.dtype)
 
 
@@ -171,13 +180,13 @@
     order = sorted_ref.shape[1]
     lane = lax.broadcasted_iota(jnp.int32, (8, LANES), 1)
     for g in range(4):
+        lags = [pltpu.roll(data_ref[p].astype(jnp.float32), (-SLOT * g) % LANES, 1) for p in range(data_ref.shape[0])]
         for tile in range(order // LANES):
             value = None
             p = (LANES * tile) // chunk
             while p < data_ref.shape[0] and chunk * p < LANES * (tile + 1):
                 begin = chunk * p - LANES * tile
-                moved = pltpu.roll(data_ref[p].astype(jnp.float32), (begin - SLOT * g) % LANES, 1)
-                value = moved if value is None else jnp.where(lane >= begin, moved, value)
+                value = lags[p] if value is None else jnp.where(lane >= begin, lags[p], value)
                 p += 1
             sorted_ref[8 * g : 8 * (g + 1), LANES * tile : LANES * (tile + 1)] = value
     bare = bare_ref[...]
@@ -189,30 +198,33 @@
     wait_in_order(refs)
 
 
-def near_kernel(parity_ref, own_ref, chip_ref, precond_ref, out_ref):
-    which = 2 - parity_ref[0]
-    out_ref[...] = jnp.dot(own_ref[...], precond_ref[0], preferred_element_type=jnp.float32) + jnp.dot(
-        chip_ref[...], precond_ref[which], preferred_element_type=jnp.float32
-    )
-
-
-def step_kernel(last, parity_ref, near_ref, far_ref, polar_ref, screened_ref, bare_ref, precond_ref, *refs):
+def times(rows, tile):
+    return jnp.dot(rows, tile, preferred_element_type=jnp.float32)
+
+
+def near_kernel(
+    first, parity_ref, own_ref, chip_ref, polar_ref, screened_ref, bare_ref, precond_ref, near_ref, base_ref
+):
+    near_ref[...] = times(own_ref[...], precond_ref[0]) + times(chip_ref[...], precond_ref[2 - parity_ref[0]])
+    bare, polar = bare_ref[...], polar_ref[...]
+    screened = jnp.broadcast_to(bare, polar.shape) if first else screened_ref[...]
+    base_ref[...] = screened + 0.5 * (bare - screened + bare * polar * screened)
+
+
+def step_kernel(last, parity_ref, near_ref, base_ref, far_ref, polar_ref, bare_ref, precond_ref, *refs):
     which = 1 + parity_ref[0]
     far = far_ref[...]
     width = 256 if last else far.shape[1]
     for at in range(0, far.shape[1], width):
         lanes = slice(at, at + width)
-        bare, polar = bare_ref[:, lanes], polar_ref[:, lanes]
-        screened = screened_ref[:, lanes] if last else jnp.broadcast_to(bare, polar.shape)
-        resid = bare - screened + bare * polar * screened
-        product = near_ref[:, lanes] + jnp.dot(far, precond_ref[which, :, lanes], preferred_element_type=jnp.float32)
-        corr = product.astype(jnp.bfloat16).astype(jnp.float32)
-        screened = screened + 0.5 * resid + corr
+        total = near_ref[:, lanes] + times(far, precond_ref[which, :, lanes])
+        screened = base_ref[:, lanes] + total.astype(jnp.bfloat16).astype(jnp.float32)
         if last:
             store_in_order(screened, refs, at)
         else:
-            refs[0][:, lanes] = screened
-            refs[1][:, lanes] = (bare - screened + bare * polar * screened).astype(jnp.bfloat16)
+            bare = bare_ref[...]
+            refs[0][...] = screened
+            refs[1][...] = (bare - screened + bare * polar_ref[...] * screened).astype(jnp.bfloat16)
     if last:
         wait_in_order(refs)
 
@@ -228,7 +240,7 @@
 
     limit = pltpu.CompilerParams(vmem_limit_bytes=VMEM_BYTES)
     matrices = [high_low(m) for m in dft_matrices(total)]
-    forward = jnp.asarray(np.stack([np.concatenate(pair, axis=1) for pair in matrices]))
+    forward = jnp.asarray(np.stack([high for high, _ in matrices]))
     backward = jnp.asarray(np.stack([np.ascontiguousarray(high.T) for high, _ in matrices]))
 
     hbm = pl.BlockSpec(memory_space=pltpu.HBM)
@@ -288,13 +300,13 @@
         last = step == ITERS - 1
         far = lax.ppermute(resid_b, "tile", far_pairs)
         chip = lax.ppermute(resid_b, "tile", chip_pairs)
-        near = pl.pallas_call(
-            near_kernel,
-            out_shape=plane,
-            in_specs=[smem] + [vmem] * 3,
-            out_specs=vmem,
+        near, base = pl.pallas_call(
+            lambda *refs, first=step == 0: near_kernel(first, *refs),
+            out_shape=(plane, plane),
+            in_specs=[smem] + [vmem] * 6,
+            out_specs=(vmem,) * 2,
             compiler_params=limit,
-        )(parity, resid_b, chip, precond)
+        )(parity, resid_b, chip, polar_sorted, screened, bare, precond)
         out = pl.pallas_call(
             lambda *refs, last=last: step_kernel(last, *refs),
             out_shape=(plane,) if last else (plane, plane_b),
@@ -302,7 +314,7 @@
             out_specs=(hbm,) if last else (vmem, vmem),
             scratch_shapes=in_order if last else [],
             compiler_params=limit,
-        )(parity, near, far, polar_sorted, screened, bare, precond)
+        )(parity, near, base, far, polar_sorted, bare, precond)
         screened = out[0]
         resid_b = out[-1]
     return (polar, screened)

time: 72.2 us -> 71.7 us (level)
  no operation moved by 1% of the time
where the time goes in v6:
time: 71.7 us; the launch traced here: 71.4 us
  blocking collectives  41.4 us (58%)
  starting transfers between devices  15.3 us (21%)
  waiting for transfers between devices  8.92 us (12%)
  Pallas kernels  4.95 us (7%)
  between operations  0.75 us (1%)
    all_to_all x1, blocking collectives, per_device(): pieces = lax.all_to_all(pieces, 'energy', 0, 0, tiled=True)  26.5 us
    all_to_all x1, blocking collectives, per_device(): lags = lax.all_to_all(lags, 'energy', 0, 0, tiled=True)  14.9 us
    ppermute x2, waiting for transfers between devices, per_device(): far = lax.ppermute(resid_b, 'tile', far_pairs)  8.91 us
    ppermute x2, starting transfers between devices, per_device(): far = lax.ppermute(resid_b, 'tile', far_pairs)  8.68 us
    ppermute x2, starting transfers between devices, per_device(): chip = lax.ppermute(resid_b, 'tile', chip_pairs)  6.66 us
    pallas_call x1, Pallas kernels, per_device(): pl.pallas_call(lambda *refs: pack_kernel(chunk, *refs), out_shape=(jax.Sh...  1.52 us
  transfers between devices with their start and end apart: 4, of which 2 were waited for; matrix products, arithmetic and copies ran while one was open for 0% of the time, Pallas kernels for 2%

profile of v6, /device:TPU:23, one launch (start us, length us, event | category | flops | bytes accessed | tf_op | source)
XLA Modules:
  0.0 71.4 jit_solution(12431257026220366737)
XLA Ops:
  0.6 0.0 copy-start.1
  0.6 0.0 copy-start
  0.7 1.5 %shard_map.77 = (bf16[24,24,128]{2,1,0:T(8,128)(2,1)S(1)}, bf16[4,384,192]{2,1,0:T(8,128)(2,1)S(1)}, bf16[4,192,384]{2,1,0:T(8,128)(2,1)S(1)}) custom-call(bf16[2,32,512]{2,1,0:T(8,128)(2,1)} %refs_0_.1, bf16[2,32,512]{2,1,0:T(8,128)(2,1)} %refs_1_.1, bf16[4,384,192]{2,1,0:T(8,128)(2,1)} %constant.21.clone.refs_2_, bf16[4,192,384]{2,1,0:T(8,128)(2,1)} %constant.22.clone.refs_3_), custom_call_target="tpu_custom_call" | custom-call | tf_op jit(solution)/shard_map/pallas_call | solution.py:250
  2.2 26.5 %all_to_all.10.refs_0_ = bf16[24,24,128]{2,1,0:T(8,128)(2,1)S(1)} all-to-all(bf16[24,24,128]{2,1,0:T(8,128)(2,1)S(1)} %get-tuple-element.13), channel_id=1, replica_groups=mesh['energy'=24,'tile'=32] {'energy'}, dimensions={0} | all-to-all | bytes 294912 | tf_op jit(solution)/shard_map/all_to_all | solution.py:262
  28.6 1.0 %shard_map.78 = bf16[24,8,128]{2,1,0:T(8,128)(2,1)S(1)} custom-call(bf16[24,24,128]{2,1,0:T(8,128)(2,1)S(1)} %all_to_all.10.refs_0_, bf16[4,384,192]{2,1,0:T(8,128)(2,1)S(1)} %get-tuple-element.14.refs_1_, bf16[4,192,384]{2,1,0:T(8,128)(2,1)S(1)} %get-tuple-element.15.refs_2_), custom_call_target="tpu_custom_call" | custom-call | tf_op jit(solution)/shard_map/pallas_call | solution.py:264
  29.7 14.9 %all_to_all.11.refs_0_ = bf16[24,8,128]{2,1,0:T(8,128)(2,1)S(1)} all-to-all(bf16[24,8,128]{2,1,0:T(8,128)(2,1)S(1)} %shard_map.78), channel_id=1, replica_groups=mesh['energy'=24,'tile'=32] {'energy'}, dimensions={0} | all-to-all | bytes 98304 | tf_op jit(solution)/shard_map/all_to_all | solution.py:271
  44.6 0.0 copy-done.1
  44.6 0.1 shard_map.79
  44.7 4.7 %collective-permute-start = (bf16[32,512]{1,0:T(8,128)(2,1)S(1)}, bf16[32,512]{1,0:T(8,128)(2,1)S(1)}, u32[]{:S(2)}, u32[]{:S(2)}) collective-permute-start(bf16[32,512]{1,0:T(8,128)(2,1)S(1)} %get-tuple-element.17.refs_1_), channel_id=1, source_target_pairs={{0,1},{1,0},{2,3},{3,2},{4,5},{5,4},{6,7},{7,6},{8,9},{9,8},{10,11... | collective-permute-start | bytes 98312 | tf_op jit(solution)/shard_map/ppermute | solution.py:302
  49.5 4.3 %collective-permute-start.1 = (bf16[32,512]{1,0:T(8,128)(2,1)S(1)}, bf16[32,512]{1,0:T(8,128)(2,1)S(1)}, u32[]{:S(2)}, u32[]{:S(2)}) collective-permute-start(bf16[32,512]{1,0:T(8,128)(2,1)S(1)} %get-tuple-element.17.refs_1_), channel_id=1, source_target_pairs={{1,2},{2,1},{3,4},{4,3},{5,6},{6,5},{7,8},{8,7},{9,10},{10,9},{11,... | collective-permute-start | bytes 98312 | tf_op jit(solution)/shard_map/ppermute | solution.py:301
  53.8 0.0 collective-permute-done.refs_2_
  53.8 0.0 copy-done
  53.8 0.3 shard_map.81
  54.1 4.8 %collective-permute-done.1.refs_3_ = bf16[32,512]{1,0:T(8,128)(2,1)S(1)} collective-permute-done((bf16[32,512]{1,0:T(8,128)(2,1)S(1)}, bf16[32,512]{1,0:T(8,128)(2,1)S(1)}, u32[]{:S(2)}, u32[]{:S(2)}) %collective-permute-start.1) | collective-permute-done | bytes 32800 | tf_op jit(solution)/shard_map/ppermute | solution.py:301
  58.9 0.2 shard_map.82
  59.1 1.9 %collective-permute-start.2 = (bf16[32,512]{1,0:T(8,128)(2,1)S(1)}, bf16[32,512]{1,0:T(8,128)(2,1)S(1)}, u32[]{:S(2)}, u32[]{:S(2)}) collective-permute-start(bf16[32,512]{1,0:T(8,128)(2,1)S(1)} %get-tuple-element.20.refs_1_), channel_id=1, source_target_pairs={{0,1},{1,0},{2,3},{3,2},{4,5},{5,4},{6,7},{7,6},{8,9},{9,8},{10,11... | collective-permute-start | bytes 98312 | tf_op jit(solution)/shard_map/ppermute | solution.py:302
  61.1 4.3 %collective-permute-start.3 = (bf16[32,512]{1,0:T(8,128)(2,1)S(1)}, bf16[32,512]{1,0:T(8,128)(2,1)S(1)}, u32[]{:S(2)}, u32[]{:S(2)}) collective-permute-start(bf16[32,512]{1,0:T(8,128)(2,1)S(1)} %get-tuple-element.20.refs_1_), channel_id=1, source_target_pairs={{1,2},{2,1},{3,4},{4,3},{5,6},{6,5},{7,8},{8,7},{9,10},{10,9},{11,... | collective-permute-start | bytes 98312 | tf_op jit(solution)/shard_map/ppermute | solution.py:301
  65.4 0.7 shard_map.80
  66.1 0.0 collective-permute-done.2.refs_2_
  66.1 0.3 shard_map.83
  66.4 4.1 %collective-permute-done.3.refs_3_ = bf16[32,512]{1,0:T(8,128)(2,1)S(1)} collective-permute-done((bf16[32,512]{1,0:T(8,128)(2,1)S(1)}, bf16[32,512]{1,0:T(8,128)(2,1)S(1)}, u32[]{:S(2)}, u32[]{:S(2)}) %collective-permute-start.3) | collective-permute-done | bytes 32800 | tf_op jit(solution)/shard_map/ppermute | solution.py:301
  70.5 0.9 %shard_map.84 = f32[32,512]{1,0:T(8,128)} custom-call(s32[1]{0:T(128)} %bitcast.1.refs_0_, f32[32,512]{1,0:T(8,128)S(1)} %get-tuple-element.22.refs_1_, f32[32,512]{1,0:T(8,128)S(1)} %get-tuple-element.23.refs_2_, bf16[32,512]{1,0:T(8,128)(2,1)S(1)} %collective-permute-done.3.refs_3_, f32[32,512]{1,0:T(8,128)S(1)} %get-tuple-element.16.sorted_ref.refs_3_.refs_4_, ...), custom_call_target="tpu_custom_call" | custom-call | tf_op jit(solution)/shard_map/pallas_call | solution.py:310
Async XLA Ops:
  0.6 44.0 %copy-start.1 = (f32[512]{0:T(512)S(1)}, f32[512]{0:T(512)}, u32[]{:S(2)}) copy-start(f32[512]{0:T(512)} %param.8) | copy-start | bytes 6148
  0.6 53.2 %copy-start = (bf16[3,512,512]{2,1,0:T(8,128)(2,1)S(1)}, bf16[3,512,512]{2,1,0:T(8,128)(2,1)}, u32[]{:S(2)}) copy-start(bf16[3,512,512]{2,1,0:T(8,128)(2,1)} %refs_6_.7) | copy-start | bytes 4718596
  44.7 9.1 %collective-permute-start = (bf16[32,512]{1,0:T(8,128)(2,1)S(1)}, bf16[32,512]{1,0:T(8,128)(2,1)S(1)}, u32[]{:S(2)}, u32[]{:S(2)}) collective-permute-start(bf16[32,512]{1,0:T(8,128)(2,1)S(1)} %get-tuple-element.17.refs_1_), channel_id=1, source_target_pairs={{0,1},{1,0},{2,3},{3,2},{4,5},{5,4},{6,7},{7,6},{8,9},{9,8},{10,11... | collective-permute-start | bytes 98312 | tf_op jit(solution)/shard_map/ppermute | solution.py:302
  49.5 9.5 %collective-permute-start.1 = (bf16[32,512]{1,0:T(8,128)(2,1)S(1)}, bf16[32,512]{1,0:T(8,128)(2,1)S(1)}, u32[]{:S(2)}, u32[]{:S(2)}) collective-permute-start(bf16[32,512]{1,0:T(8,128)(2,1)S(1)} %get-tuple-element.17.refs_1_), channel_id=1, source_target_pairs={{1,2},{2,1},{3,4},{4,3},{5,6},{6,5},{7,8},{8,7},{9,10},{10,9},{11,... | collective-permute-start | bytes 98312 | tf_op jit(solution)/shard_map/ppermute | solution.py:301
  59.1 6.9 %collective-permute-start.2 = (bf16[32,512]{1,0:T(8,128)(2,1)S(1)}, bf16[32,512]{1,0:T(8,128)(2,1)S(1)}, u32[]{:S(2)}, u32[]{:S(2)}) collective-permute-start(bf16[32,512]{1,0:T(8,128)(2,1)S(1)} %get-tuple-element.20.refs_1_), channel_id=1, source_target_pairs={{0,1},{1,0},{2,3},{3,2},{4,5},{5,4},{6,7},{7,6},{8,9},{9,8},{10,11... | collective-permute-start | bytes 98312 | tf_op jit(solution)/shard_map/ppermute | solution.py:302
  61.1 9.5 %collective-permute-start.3 = (bf16[32,512]{1,0:T(8,128)(2,1)S(1)}, bf16[32,512]{1,0:T(8,128)(2,1)S(1)}, u32[]{:S(2)}, u32[]{:S(2)}) collective-permute-start(bf16[32,512]{1,0:T(8,128)(2,1)S(1)} %get-tuple-element.20.refs_1_), channel_id=1, source_target_pairs={{1,2},{2,1},{3,4},{4,3},{5,6},{6,5},{7,8},{8,7},{9,10},{10,9},{11,... | collective-permute-start | bytes 98312 | tf_op jit(solution)/shard_map/ppermute | solution.py:301

commit v7 on v6

--- a/solution.py
+++ b/solution.py
@@ -38,31 +38,37 @@
     copies = [
         pltpu.make_async_copy(src, dst, sems.at[n])
         for n, (src, dst) in enumerate(
-            ((less_hbm, less_ref), (great_hbm, great_ref), (fwd_hbm, fwd_ref), (back_hbm, back_ref))
+            (
+                (less_hbm.at[0], less_ref.at[0]),
+                (less_hbm.at[1], less_ref.at[1]),
+                (great_hbm.at[0], great_ref.at[0]),
+                (great_hbm.at[1], great_ref.at[1]),
+                (fwd_hbm, fwd_ref),
+                (back_hbm, back_ref),
+            )
         )
     ]
     for copy in copies:
         copy.start()
     e_dev, order = less_ref.shape[1], less_ref.shape[2]
-    row = lax.broadcasted_iota(jnp.int32, (4 * e_dev, 4 * e_dev), 0)
-    col = lax.broadcasted_iota(jnp.int32, (4 * e_dev, 4 * e_dev), 1)
-    inner = row % e_dev
-    source = row - inner + 4 * (inner % 8) + inner // 8
+    row = lax.broadcasted_iota(jnp.int32, (e_dev, e_dev), 0)
+    col = lax.broadcasted_iota(jnp.int32, (e_dev, e_dev), 1)
+    source = 4 * (row % 8) + row // 8
     select = jnp.where(col == source, 1.0, 0.0).astype(jnp.bfloat16)
     lane = lax.broadcasted_iota(jnp.int32, (8, LANES), 1)
     spare = SLOT - chunk
-    copies[0].wait()
-    copies[1].wait()
-    rows = jnp.concatenate([less_ref[0], less_ref[1], great_ref[0], great_ref[1]], axis=0)
-    sorted_rows = jnp.dot(select, rows, preferred_element_type=jnp.float32)
 
     def moved(q, r, tile, shift):
-        part = sorted_rows[e_dev * q + 8 * r : e_dev * q + 8 * (r + 1), LANES * tile : LANES * (tile + 1)]
+        part = ordered[q][8 * r : 8 * (r + 1), LANES * tile : LANES * (tile + 1)]
         return pltpu.roll(part, shift % LANES, 1) if shift % LANES else part
 
     tiles = range(order // LANES)
-    main = [[[moved(q, g, t, SLOT * q) for t in tiles] for g in range(3)] for q in range(4)]
-    rest = [[[moved(q, 3, t, SLOT * q + chunk - spare * g) for t in tiles] for g in range(3)] for q in range(4)]
+    ordered, main, rest = [], [], []
+    for q, ref in enumerate((less_ref.at[0], less_ref.at[1], great_ref.at[0], great_ref.at[1])):
+        copies[q].wait()
+        ordered.append(jnp.dot(select, ref[...], preferred_element_type=jnp.float32))
+        main.append([[moved(q, g, t, SLOT * q) for t in tiles] for g in range(3)])
+        rest.append([[moved(q, 3, t, SLOT * q + chunk - spare * g) for t in tiles] for g in range(3)])
     for p in range(out_ref.shape[0]):
         low = chunk * p
         first, last = low // LANES, (min(low + chunk, order) - 1) // LANES
@@ -84,8 +90,8 @@
                 extra = jnp.where(inner - chunk + spare * g >= LANES - turn, chain(rest, g, last), extra)
             groups.append(jnp.where(inner < chunk, ours, extra))
         out_ref[p] = jnp.concatenate(groups, axis=0).astype(jnp.bfloat16)
-    copies[2].wait()
-    copies[3].wait()
+    copies[4].wait()
+    copies[5].wait()
 
 
 def product(a, b):
@@ -256,7 +262,7 @@
         ),
         in_specs=[hbm] * 4,
         out_specs=(vmem,) * 3,
-        scratch_shapes=[pltpu.VMEM(g_less.shape, jnp.bfloat16)] * 2 + [pltpu.SemaphoreType.DMA((4,))],
+        scratch_shapes=[pltpu.VMEM(g_less.shape, jnp.bfloat16)] * 2 + [pltpu.SemaphoreType.DMA((6,))],
         compiler_params=limit,
     )(g_less, g_great, forward, backward)
     pieces = lax.all_to_all(pieces, "energy", 0, 0, tiled=True)

time: 71.7 us -> 71.9 us (level)
  no operation moved by 1% of the time
where the time goes in v7:
time: 71.9 us; the launch traced here: 71.7 us
  blocking collectives  41.4 us (58%)
  starting transfers between devices  15.3 us (21%)
  waiting for transfers between devices  8.92 us (12%)
  Pallas kernels  5.27 us (7%)
  between operations  0.75 us (1%)
    all_to_all x1, blocking collectives, per_device(): pieces = lax.all_to_all(pieces, 'energy', 0, 0, tiled=True)  26.5 us
    all_to_all x1, blocking collectives, per_device(): lags = lax.all_to_all(lags, 'energy', 0, 0, tiled=True)  14.9 us
    ppermute x2, waiting for transfers between devices, per_device(): far = lax.ppermute(resid_b, 'tile', far_pairs)  8.91 us
    ppermute x2, starting transfers between devices, per_device(): far = lax.ppermute(resid_b, 'tile', far_pairs)  8.68 us
    ppermute x2, starting transfers between devices, per_device(): chip = lax.ppermute(resid_b, 'tile', chip_pairs)  6.64 us
    pallas_call x1, Pallas kernels, per_device(): pl.pallas_call(lambda *refs: pack_kernel(chunk, *refs), out_shape=(jax.Sh...  1.84 us
  transfers between devices with their start and end apart: 4, of which 2 were waited for; matrix products, arithmetic and copies ran while one was open for 0% of the time, Pallas kernels for 2%

profile of v7, /device:TPU:23, one launch (start us, length us, event | category | flops | bytes accessed | tf_op | source)
XLA Modules:
  0.0 71.7 jit_solution(15146141229912621159)
XLA Ops:
  0.6 0.0 copy-start.1
  0.6 0.0 copy-start
  0.7 1.8 %shard_map.77 = (bf16[24,24,128]{2,1,0:T(8,128)(2,1)S(1)}, bf16[4,384,192]{2,1,0:T(8,128)(2,1)S(1)}, bf16[4,192,384]{2,1,0:T(8,128)(2,1)S(1)}) custom-call(bf16[2,32,512]{2,1,0:T(8,128)(2,1)} %refs_0_.1, bf16[2,32,512]{2,1,0:T(8,128)(2,1)} %refs_1_.1, bf16[4,384,192]{2,1,0:T(8,128)(2,1)} %constant.21.clone.refs_2_, bf16[4,192,384]{2,1,0:T(8,128)(2,1)} %constant.22.clone.refs_3_), custom_call_target="tpu_custom_call" | custom-call | tf_op jit(solution)/shard_map/pallas_call | solution.py:256
  2.5 26.5 %all_to_all.10.refs_0_ = bf16[24,24,128]{2,1,0:T(8,128)(2,1)S(1)} all-to-all(bf16[24,24,128]{2,1,0:T(8,128)(2,1)S(1)} %get-tuple-element.13), channel_id=1, replica_groups=mesh['energy'=24,'tile'=32] {'energy'}, dimensions={0} | all-to-all | bytes 294912 | tf_op jit(solution)/shard_map/all_to_all | solution.py:268
  29.0 1.0 %shard_map.78 = bf16[24,8,128]{2,1,0:T(8,128)(2,1)S(1)} custom-call(bf16[24,24,128]{2,1,0:T(8,128)(2,1)S(1)} %all_to_all.10.refs_0_, bf16[4,384,192]{2,1,0:T(8,128)(2,1)S(1)} %get-tuple-element.14.refs_1_, bf16[4,192,384]{2,1,0:T(8,128)(2,1)S(1)} %get-tuple-element.15.refs_2_), custom_call_target="tpu_custom_call" | custom-call | tf_op jit(solution)/shard_map/pallas_call | solution.py:270
  30.0 14.9 %all_to_all.11.refs_0_ = bf16[24,8,128]{2,1,0:T(8,128)(2,1)S(1)} all-to-all(bf16[24,8,128]{2,1,0:T(8,128)(2,1)S(1)} %shard_map.78), channel_id=1, replica_groups=mesh['energy'=24,'tile'=32] {'energy'}, dimensions={0} | all-to-all | bytes 98304 | tf_op jit(solution)/shard_map/all_to_all | solution.py:277
  44.9 0.0 copy-done.1
  44.9 0.1 shard_map.79
  45.0 4.7 %collective-permute-start = (bf16[32,512]{1,0:T(8,128)(2,1)S(1)}, bf16[32,512]{1,0:T(8,128)(2,1)S(1)}, u32[]{:S(2)}, u32[]{:S(2)}) collective-permute-start(bf16[32,512]{1,0:T(8,128)(2,1)S(1)} %get-tuple-element.17.refs_1_), channel_id=1, source_target_pairs={{0,1},{1,0},{2,3},{3,2},{4,5},{5,4},{6,7},{7,6},{8,9},{9,8},{10,11... | collective-permute-start | bytes 98312 | tf_op jit(solution)/shard_map/ppermute | solution.py:308
  49.8 4.3 %collective-permute-start.1 = (bf16[32,512]{1,0:T(8,128)(2,1)S(1)}, bf16[32,512]{1,0:T(8,128)(2,1)S(1)}, u32[]{:S(2)}, u32[]{:S(2)}) collective-permute-start(bf16[32,512]{1,0:T(8,128)(2,1)S(1)} %get-tuple-element.17.refs_1_), channel_id=1, source_target_pairs={{1,2},{2,1},{3,4},{4,3},{5,6},{6,5},{7,8},{8,7},{9,10},{10,9},{11,... | collective-permute-start | bytes 98312 | tf_op jit(solution)/shard_map/ppermute | solution.py:307
  54.1 0.0 collective-permute-done.refs_2_
  54.1 0.0 copy-done
  54.1 0.3 shard_map.81
  54.4 4.8 %collective-permute-done.1.refs_3_ = bf16[32,512]{1,0:T(8,128)(2,1)S(1)} collective-permute-done((bf16[32,512]{1,0:T(8,128)(2,1)S(1)}, bf16[32,512]{1,0:T(8,128)(2,1)S(1)}, u32[]{:S(2)}, u32[]{:S(2)}) %collective-permute-start.1) | collective-permute-done | bytes 32800 | tf_op jit(solution)/shard_map/ppermute | solution.py:307
  59.2 0.2 shard_map.82
  59.4 1.9 %collective-permute-start.2 = (bf16[32,512]{1,0:T(8,128)(2,1)S(1)}, bf16[32,512]{1,0:T(8,128)(2,1)S(1)}, u32[]{:S(2)}, u32[]{:S(2)}) collective-permute-start(bf16[32,512]{1,0:T(8,128)(2,1)S(1)} %get-tuple-element.20.refs_1_), channel_id=1, source_target_pairs={{0,1},{1,0},{2,3},{3,2},{4,5},{5,4},{6,7},{7,6},{8,9},{9,8},{10,11... | collective-permute-start | bytes 98312 | tf_op jit(solution)/shard_map/ppermute | solution.py:308
  61.4 4.3 %collective-permute-start.3 = (bf16[32,512]{1,0:T(8,128)(2,1)S(1)}, bf16[32,512]{1,0:T(8,128)(2,1)S(1)}, u32[]{:S(2)}, u32[]{:S(2)}) collective-permute-start(bf16[32,512]{1,0:T(8,128)(2,1)S(1)} %get-tuple-element.20.refs_1_), channel_id=1, source_target_pairs={{1,2},{2,1},{3,4},{4,3},{5,6},{6,5},{7,8},{8,7},{9,10},{10,9},{11,... | collective-permute-start | bytes 98312 | tf_op jit(solution)/shard_map/ppermute | solution.py:307
  65.7 0.7 shard_map.80
  66.4 0.0 collective-permute-done.2.refs_2_
  66.4 0.3 shard_map.83
  66.7 4.1 %collective-permute-done.3.refs_3_ = bf16[32,512]{1,0:T(8,128)(2,1)S(1)} collective-permute-done((bf16[32,512]{1,0:T(8,128)(2,1)S(1)}, bf16[32,512]{1,0:T(8,128)(2,1)S(1)}, u32[]{:S(2)}, u32[]{:S(2)}) %collective-permute-start.3) | collective-permute-done | bytes 32800 | tf_op jit(solution)/shard_map/ppermute | solution.py:307
  70.8 0.9 %shard_map.84 = f32[32,512]{1,0:T(8,128)} custom-call(s32[1]{0:T(128)} %bitcast.1.refs_0_, f32[32,512]{1,0:T(8,128)S(1)} %get-tuple-element.22.refs_1_, f32[32,512]{1,0:T(8,128)S(1)} %get-tuple-element.23.refs_2_, bf16[32,512]{1,0:T(8,128)(2,1)S(1)} %collective-permute-done.3.refs_3_, f32[32,512]{1,0:T(8,128)S(1)} %get-tuple-element.16.sorted_ref.refs_3_.refs_4_, ...), custom_call_target="tpu_custom_call" | custom-call | tf_op jit(solution)/shard_map/pallas_call | solution.py:316
Async XLA Ops:
  0.6 44.3 %copy-start.1 = (f32[512]{0:T(512)S(1)}, f32[512]{0:T(512)}, u32[]{:S(2)}) copy-start(f32[512]{0:T(512)} %param.8) | copy-start | bytes 6148
  0.6 53.5 %copy-start = (bf16[3,512,512]{2,1,0:T(8,128)(2,1)S(1)}, bf16[3,512,512]{2,1,0:T(8,128)(2,1)}, u32[]{:S(2)}) copy-start(bf16[3,512,512]{2,1,0:T(8,128)(2,1)} %refs_6_.7) | copy-start | bytes 4718596
  45.0 9.1 %collective-permute-start = (bf16[32,512]{1,0:T(8,128)(2,1)S(1)}, bf16[32,512]{1,0:T(8,128)(2,1)S(1)}, u32[]{:S(2)}, u32[]{:S(2)}) collective-permute-start(bf16[32,512]{1,0:T(8,128)(2,1)S(1)} %get-tuple-element.17.refs_1_), channel_id=1, source_target_pairs={{0,1},{1,0},{2,3},{3,2},{4,5},{5,4},{6,7},{7,6},{8,9},{9,8},{10,11... | collective-permute-start | bytes 98312 | tf_op jit(solution)/shard_map/ppermute | solution.py:308
  49.8 9.5 %collective-permute-start.1 = (bf16[32,512]{1,0:T(8,128)(2,1)S(1)}, bf16[32,512]{1,0:T(8,128)(2,1)S(1)}, u32[]{:S(2)}, u32[]{:S(2)}) collective-permute-start(bf16[32,512]{1,0:T(8,128)(2,1)S(1)} %get-tuple-element.17.refs_1_), channel_id=1, source_target_pairs={{1,2},{2,1},{3,4},{4,3},{5,6},{6,5},{7,8},{8,7},{9,10},{10,9},{11,... | collective-permute-start | bytes 98312 | tf_op jit(solution)/shard_map/ppermute | solution.py:307
  59.4 6.9 %collective-permute-start.2 = (bf16[32,512]{1,0:T(8,128)(2,1)S(1)}, bf16[32,512]{1,0:T(8,128)(2,1)S(1)}, u32[]{:S(2)}, u32[]{:S(2)}) collective-permute-start(bf16[32,512]{1,0:T(8,128)(2,1)S(1)} %get-tuple-element.20.refs_1_), channel_id=1, source_target_pairs={{0,1},{1,0},{2,3},{3,2},{4,5},{5,4},{6,7},{7,6},{8,9},{9,8},{10,11... | collective-permute-start | bytes 98312 | tf_op jit(solution)/shard_map/ppermute | solution.py:308
  61.4 9.5 %collective-permute-start.3 = (bf16[32,512]{1,0:T(8,128)(2,1)S(1)}, bf16[32,512]{1,0:T(8,128)(2,1)S(1)}, u32[]{:S(2)}, u32[]{:S(2)}) collective-permute-start(bf16[32,512]{1,0:T(8,128)(2,1)S(1)} %get-tuple-element.20.refs_1_), channel_id=1, source_target_pairs={{1,2},{2,1},{3,4},{4,3},{5,6},{6,5},{7,8},{8,7},{9,10},{10,9},{11,... | collective-permute-start | bytes 98312 | tf_op jit(solution)/shard_map/ppermute | solution.py:307

commit v8 on v6

--- a/solution.py
+++ b/solution.py
@@ -179,18 +179,27 @@
 def unpack_kernel(chunk, data_ref, bare_ref, sorted_ref, resid_ref):
     order = sorted_ref.shape[1]
     lane = lax.broadcasted_iota(jnp.int32, (8, LANES), 1)
-    for g in range(4):
-        lags = [pltpu.roll(data_ref[p].astype(jnp.float32), (-SLOT * g) % LANES, 1) for p in range(data_ref.shape[0])]
+    bare = bare_ref[...]
+    for half in range(2):
+        lags = [
+            [pltpu.roll(data_ref[p].astype(jnp.float32), (-SLOT * g) % LANES, 1) for p in range(data_ref.shape[0])]
+            for g in (2 * half, 2 * half + 1)
+        ]
+        rows = slice(16 * half, 16 * (half + 1))
         for tile in range(order // LANES):
-            value = None
-            p = (LANES * tile) // chunk
-            while p < data_ref.shape[0] and chunk * p < LANES * (tile + 1):
-                begin = chunk * p - LANES * tile
-                value = lags[p] if value is None else jnp.where(lane >= begin, lags[p], value)
-                p += 1
-            sorted_ref[8 * g : 8 * (g + 1), LANES * tile : LANES * (tile + 1)] = value
-    bare = bare_ref[...]
-    resid_ref[...] = (bare * sorted_ref[...] * bare).astype(jnp.bfloat16)
+            lanes = slice(LANES * tile, LANES * (tile + 1))
+            values = []
+            for pieces in lags:
+                value = None
+                p = (LANES * tile) // chunk
+                while p < data_ref.shape[0] and chunk * p < LANES * (tile + 1):
+                    begin = chunk * p - LANES * tile
+                    value = pieces[p] if value is None else jnp.where(lane >= begin, pieces[p], value)
+                    p += 1
+                values.append(value)
+            value = jnp.concatenate(values, axis=0)
+            sorted_ref[rows, lanes] = value
+            resid_ref[rows, lanes] = (bare[:, lanes] * value * bare[:, lanes]).astype(jnp.bfloat16)
 
 
 def order_kernel(sorted_ref, *refs):

time: 71.7 us -> 71.7 us (level)
  no operation moved by 1% of the time
where the time goes in v8:
time: 71.7 us; the launch traced here: 71.4 us
  blocking collectives  41.4 us (58%)
  starting transfers between devices  15.3 us (21%)
  waiting for transfers between devices  8.92 us (12%)
  Pallas kernels  4.95 us (7%)
  between operations  0.75 us (1%)
    all_to_all x1, blocking collectives, per_device(): pieces = lax.all_to_all(pieces, 'energy', 0, 0, tiled=True)  26.5 us
    all_to_all x1, blocking collectives, per_device(): lags = lax.all_to_all(lags, 'energy', 0, 0, tiled=True)  14.9 us
    ppermute x2, waiting for transfers between devices, per_device(): far = lax.ppermute(resid_b, 'tile', far_pairs)  8.91 us
    ppermute x2, starting transfers between devices, per_device(): far = lax.ppermute(resid_b, 'tile', far_pairs)  8.68 us
    ppermute x2, starting transfers between devices, per_device(): chip = lax.ppermute(resid_b, 'tile', chip_pairs)  6.66 us
    pallas_call x1, Pallas kernels, per_device(): pl.pallas_call(lambda *refs: pack_kernel(chunk, *refs), out_shape=(jax.Sh...  1.52 us
  transfers between devices with their start and end apart: 4, of which 2 were waited for; matrix products, arithmetic and copies ran while one was open for 0% of the time, Pallas kernels for 2%

profile of v8, /device:TPU:23, one launch (start us, length us, event | category | flops | bytes accessed | tf_op | source)
XLA Modules:
  0.0 71.4 jit_solution(8189275014119803139)
XLA Ops:
  0.6 0.0 copy-start.1
  0.6 0.0 copy-start
  0.7 1.5 %shard_map.77 = (bf16[24,24,128]{2,1,0:T(8,128)(2,1)S(1)}, bf16[4,384,192]{2,1,0:T(8,128)(2,1)S(1)}, bf16[4,192,384]{2,1,0:T(8,128)(2,1)S(1)}) custom-call(bf16[2,32,512]{2,1,0:T(8,128)(2,1)} %refs_0_.1, bf16[2,32,512]{2,1,0:T(8,128)(2,1)} %refs_1_.1, bf16[4,384,192]{2,1,0:T(8,128)(2,1)} %constant.21.clone.refs_2_, bf16[4,192,384]{2,1,0:T(8,128)(2,1)} %constant.22.clone.refs_3_), custom_call_target="tpu_custom_call" | custom-call | tf_op jit(solution)/shard_map/pallas_call | solution.py:259
  2.2 26.5 %all_to_all.10.refs_0_ = bf16[24,24,128]{2,1,0:T(8,128)(2,1)S(1)} all-to-all(bf16[24,24,128]{2,1,0:T(8,128)(2,1)S(1)} %get-tuple-element.13), channel_id=1, replica_groups=mesh['energy'=24,'tile'=32] {'energy'}, dimensions={0} | all-to-all | bytes 294912 | tf_op jit(solution)/shard_map/all_to_all | solution.py:271
  28.6 1.0 %shard_map.78 = bf16[24,8,128]{2,1,0:T(8,128)(2,1)S(1)} custom-call(bf16[24,24,128]{2,1,0:T(8,128)(2,1)S(1)} %all_to_all.10.refs_0_, bf16[4,384,192]{2,1,0:T(8,128)(2,1)S(1)} %get-tuple-element.14.refs_1_, bf16[4,192,384]{2,1,0:T(8,128)(2,1)S(1)} %get-tuple-element.15.refs_2_), custom_call_target="tpu_custom_call" | custom-call | tf_op jit(solution)/shard_map/pallas_call | solution.py:273
  29.7 14.9 %all_to_all.11.refs_0_ = bf16[24,8,128]{2,1,0:T(8,128)(2,1)S(1)} all-to-all(bf16[24,8,128]{2,1,0:T(8,128)(2,1)S(1)} %shard_map.78), channel_id=1, replica_groups=mesh['energy'=24,'tile'=32] {'energy'}, dimensions={0} | all-to-all | bytes 98304 | tf_op jit(solution)/shard_map/all_to_all | solution.py:280
  44.6 0.0 copy-done.1
  44.6 0.1 shard_map.79
  44.7 4.7 %collective-permute-start = (bf16[32,512]{1,0:T(8,128)(2,1)S(1)}, bf16[32,512]{1,0:T(8,128)(2,1)S(1)}, u32[]{:S(2)}, u32[]{:S(2)}) collective-permute-start(bf16[32,512]{1,0:T(8,128)(2,1)S(1)} %get-tuple-element.17.refs_1_), channel_id=1, source_target_pairs={{0,1},{1,0},{2,3},{3,2},{4,5},{5,4},{6,7},{7,6},{8,9},{9,8},{10,11... | collective-permute-start | bytes 98312 | tf_op jit(solution)/shard_map/ppermute | solution.py:311
  49.5 4.3 %collective-permute-start.1 = (bf16[32,512]{1,0:T(8,128)(2,1)S(1)}, bf16[32,512]{1,0:T(8,128)(2,1)S(1)}, u32[]{:S(2)}, u32[]{:S(2)}) collective-permute-start(bf16[32,512]{1,0:T(8,128)(2,1)S(1)} %get-tuple-element.17.refs_1_), channel_id=1, source_target_pairs={{1,2},{2,1},{3,4},{4,3},{5,6},{6,5},{7,8},{8,7},{9,10},{10,9},{11,... | collective-permute-start | bytes 98312 | tf_op jit(solution)/shard_map/ppermute | solution.py:310
  53.8 0.0 collective-permute-done.refs_2_
  53.8 0.0 copy-done
  53.8 0.3 shard_map.81
  54.1 4.8 %collective-permute-done.1.refs_3_ = bf16[32,512]{1,0:T(8,128)(2,1)S(1)} collective-permute-done((bf16[32,512]{1,0:T(8,128)(2,1)S(1)}, bf16[32,512]{1,0:T(8,128)(2,1)S(1)}, u32[]{:S(2)}, u32[]{:S(2)}) %collective-permute-start.1) | collective-permute-done | bytes 32800 | tf_op jit(solution)/shard_map/ppermute | solution.py:310
  58.9 0.2 shard_map.82
  59.1 1.9 %collective-permute-start.2 = (bf16[32,512]{1,0:T(8,128)(2,1)S(1)}, bf16[32,512]{1,0:T(8,128)(2,1)S(1)}, u32[]{:S(2)}, u32[]{:S(2)}) collective-permute-start(bf16[32,512]{1,0:T(8,128)(2,1)S(1)} %get-tuple-element.20.refs_1_), channel_id=1, source_target_pairs={{0,1},{1,0},{2,3},{3,2},{4,5},{5,4},{6,7},{7,6},{8,9},{9,8},{10,11... | collective-permute-start | bytes 98312 | tf_op jit(solution)/shard_map/ppermute | solution.py:311
  61.1 4.3 %collective-permute-start.3 = (bf16[32,512]{1,0:T(8,128)(2,1)S(1)}, bf16[32,512]{1,0:T(8,128)(2,1)S(1)}, u32[]{:S(2)}, u32[]{:S(2)}) collective-permute-start(bf16[32,512]{1,0:T(8,128)(2,1)S(1)} %get-tuple-element.20.refs_1_), channel_id=1, source_target_pairs={{1,2},{2,1},{3,4},{4,3},{5,6},{6,5},{7,8},{8,7},{9,10},{10,9},{11,... | collective-permute-start | bytes 98312 | tf_op jit(solution)/shard_map/ppermute | solution.py:310
  65.4 0.7 shard_map.80
  66.1 0.0 collective-permute-done.2.refs_2_
  66.1 0.3 shard_map.83
  66.4 4.1 %collective-permute-done.3.refs_3_ = bf16[32,512]{1,0:T(8,128)(2,1)S(1)} collective-permute-done((bf16[32,512]{1,0:T(8,128)(2,1)S(1)}, bf16[32,512]{1,0:T(8,128)(2,1)S(1)}, u32[]{:S(2)}, u32[]{:S(2)}) %collective-permute-start.3) | collective-permute-done | bytes 32800 | tf_op jit(solution)/shard_map/ppermute | solution.py:310
  70.5 0.9 %shard_map.84 = f32[32,512]{1,0:T(8,128)} custom-call(s32[1]{0:T(128)} %bitcast.1.refs_0_, f32[32,512]{1,0:T(8,128)S(1)} %get-tuple-element.22.refs_1_, f32[32,512]{1,0:T(8,128)S(1)} %get-tuple-element.23.refs_2_, bf16[32,512]{1,0:T(8,128)(2,1)S(1)} %collective-permute-done.3.refs_3_, f32[32,512]{1,0:T(8,128)S(1)} %get-tuple-element.16.sorted_ref.refs_3_.refs_4_, ...), custom_call_target="tpu_custom_call" | custom-call | tf_op jit(solution)/shard_map/pallas_call | solution.py:319
Async XLA Ops:
  0.6 44.0 %copy-start.1 = (f32[512]{0:T(512)S(1)}, f32[512]{0:T(512)}, u32[]{:S(2)}) copy-start(f32[512]{0:T(512)} %param.8) | copy-start | bytes 6148
  0.6 53.2 %copy-start = (bf16[3,512,512]{2,1,0:T(8,128)(2,1)S(1)}, bf16[3,512,512]{2,1,0:T(8,128)(2,1)}, u32[]{:S(2)}) copy-start(bf16[3,512,512]{2,1,0:T(8,128)(2,1)} %refs_6_.7) | copy-start | bytes 4718596
  44.7 9.1 %collective-permute-start = (bf16[32,512]{1,0:T(8,128)(2,1)S(1)}, bf16[32,512]{1,0:T(8,128)(2,1)S(1)}, u32[]{:S(2)}, u32[]{:S(2)}) collective-permute-start(bf16[32,512]{1,0:T(8,128)(2,1)S(1)} %get-tuple-element.17.refs_1_), channel_id=1, source_target_pairs={{0,1},{1,0},{2,3},{3,2},{4,5},{5,4},{6,7},{7,6},{8,9},{9,8},{10,11... | collective-permute-start | bytes 98312 | tf_op jit(solution)/shard_map/ppermute | solution.py:311
  49.5 9.5 %collective-permute-start.1 = (bf16[32,512]{1,0:T(8,128)(2,1)S(1)}, bf16[32,512]{1,0:T(8,128)(2,1)S(1)}, u32[]{:S(2)}, u32[]{:S(2)}) collective-permute-start(bf16[32,512]{1,0:T(8,128)(2,1)S(1)} %get-tuple-element.17.refs_1_), channel_id=1, source_target_pairs={{1,2},{2,1},{3,4},{4,3},{5,6},{6,5},{7,8},{8,7},{9,10},{10,9},{11,... | collective-permute-start | bytes 98312 | tf_op jit(solution)/shard_map/ppermute | solution.py:310
  59.1 6.9 %collective-permute-start.2 = (bf16[32,512]{1,0:T(8,128)(2,1)S(1)}, bf16[32,512]{1,0:T(8,128)(2,1)S(1)}, u32[]{:S(2)}, u32[]{:S(2)}) collective-permute-start(bf16[32,512]{1,0:T(8,128)(2,1)S(1)} %get-tuple-element.20.refs_1_), channel_id=1, source_target_pairs={{0,1},{1,0},{2,3},{3,2},{4,5},{5,4},{6,7},{7,6},{8,9},{9,8},{10,11... | collective-permute-start | bytes 98312 | tf_op jit(solution)/shard_map/ppermute | solution.py:311
  61.1 9.5 %collective-permute-start.3 = (bf16[32,512]{1,0:T(8,128)(2,1)S(1)}, bf16[32,512]{1,0:T(8,128)(2,1)S(1)}, u32[]{:S(2)}, u32[]{:S(2)}) collective-permute-start(bf16[32,512]{1,0:T(8,128)(2,1)S(1)} %get-tuple-element.20.refs_1_), channel_id=1, source_target_pairs={{1,2},{2,1},{3,4},{4,3},{5,6},{6,5},{7,8},{8,7},{9,10},{10,9},{11,... | collective-permute-start | bytes 98312 | tf_op jit(solution)/shard_map/ppermute | solution.py:310
